TPU v7x, 1024 devices: a whole 8x8x8 slice. The times are simulated.
1024 devices in a mesh: lon: 32 (over y_lo, z, core), colat: 32 (over x, y_hi).
Axes of the slice: x: 8, y: 8 (y_hi: 4, y_lo: 2; y = y_hi * 2 + y_lo), z: 8, core: 2. Of those that a mesh axis runs over, the one named last changes fastest.
Arguments:
- forward_state: float32 [9, 8, 512, 4096], P(None, None, 'colat', 'lon'), may hold values from -6 to 6
- adjoint_state: float32 [9, 8, 512, 4096], P(None, None, 'colat', 'lon'), may hold values from -6 to 6
- layer_ids: int32 [8, 512, 4096], P(None, 'colat', 'lon'), may hold values from 0 to 15
- density_table: float32 [16], replicated, may hold values from 2 to 4
- lame_table: float32 [16], replicated, may hold values from 0.5 to 2
- shear_table: float32 [16], replicated, may hold values from 0.5 to 1.5
- source_cells: int32 [8], replicated, may hold values from 0 to 16777215
- source_wavelet: float32 [2, 8], replicated, may hold values from -6 to 6
- receiver_cells: int32 [512], replicated, may hold values from 0 to 16777215
- receiver_residual: float32 [2, 3, 512], replicated, may hold values from -6 to 6
Outputs:
- forward_field: float32 [9, 8, 512, 4096], P(None, None, 'colat', 'lon')
- adjoint_field: float32 [9, 8, 512, 4096], P(None, None, 'colat', 'lon')
- density_kernel: float32 [8, 512, 4096], P(None, 'colat', 'lon')
Inputs may be any that keep to these rules, and one draw needn't show every extreme that they name: `source_cells`: flat index (level * 512 + colatitude) * 4096 + longitude. `receiver_cells`: flat index as for the sources.
All inputs are finite; a program needn't handle non-finite values.
Results may differ from a plain program's by a relative error of at most 0.0001.
Values sent between devices are 32-bit elements; how exact they have to be, the bound alone decides.
A program may use at most 32 MiB of HBM per device.

v0:
```python
import math

import jax
import jax.numpy as jnp
from jax import lax
from jax.sharding import PartitionSpec as P

STEPS = 2


R_INNER = 0.55
COURANT = 0.3
SIN_FLOOR = 0.25
VEL_SIGNS = (-1.0, -1.0, 1.0)
STRESS_SIGNS = (1.0, 1.0, 1.0, 1.0, -1.0, -1.0)


def from_behind(value, axis, steps):
    count = lax.axis_size(axis)
    pairs = [(source, (source + steps) % count) for source in range(count)]
    return lax.ppermute(value, axis, pairs)


def extended(array, sides, width, wrap):
    for axis, dim in sides:
        peers, length = (lax.axis_size(axis), array.shape[dim])
        up = [(i, (i + 1) % peers) for i in range(peers if wrap else peers - 1)]
        down = [(j, i) for i, j in up]
        last = lax.slice_in_dim(array, length - width, length, axis=dim)
        leading = lax.slice_in_dim(array, 0, width, axis=dim)
        before = lax.ppermute(last, axis, up)
        after = lax.ppermute(leading, axis, down)
        array = jnp.concatenate([before, array, after], axis=dim)
    return array


def geometry(row_ids, levels, lat_cells, lon_cells):
    theta_step = math.pi / lat_cells
    phi_step = 2.0 * math.pi / lon_cells
    delta_r = (1.0 - R_INNER) / levels
    radius = R_INNER + (jnp.arange(levels, dtype=jnp.float32) + 0.5) * delta_r
    colatitude = (row_ids.astype(jnp.float32) + 0.5) * theta_step
    sines_held = jnp.maximum(jnp.sin(colatitude), SIN_FLOOR)
    cotangent = jnp.cos(colatitude) / sines_held
    inv_radius = (1.0 / radius)[:, None, None]
    along_theta = inv_radius / theta_step
    along_phi = inv_radius / (sines_held[None, :, None] * phi_step)
    curvature = cotangent[None, :, None] * inv_radius
    return (along_theta, along_phi, curvature, inv_radius, 1.0 / delta_r)


def time_step(lon_cells):
    return COURANT * SIN_FLOOR * R_INNER * (2.0 * math.pi / lon_cells) / 1.6


def diff_theta(values):
    return (
        8.0 * (values[..., 3:-1, 2:-2] - values[..., 1:-3, 2:-2])
        - (values[..., 4:, 2:-2] - values[..., :-4, 2:-2])
    ) / 12.0


def diff_phi(values):
    return (
        8.0 * (values[..., 2:-2, 3:-1] - values[..., 2:-2, 1:-3])
        - (values[..., 2:-2, 4:] - values[..., 2:-2, :-4])
    ) / 12.0


def diff_radial(values):
    padded = jnp.pad(values, [(0, 0)] * (values.ndim - 3) + [(1, 1), (0, 0), (0, 0)])
    return (padded[..., 2:, :, :] - padded[..., :-2, :, :]) * 0.5


def accelerate(stress, metric):
    along_theta, along_phi, curvature, inv_radius, inv_spacing = metric
    centre_part = stress[..., 2:-2, 2:-2]
    stress_tt, stress_pp, stress_rr = (centre_part[:, 0], centre_part[:, 1], centre_part[:, 2])
    stress_tp, stress_tr, stress_pr = (centre_part[:, 3], centre_part[:, 4], centre_part[:, 5])
    theta_diff = diff_theta(stress)
    phi_diff = diff_phi(stress)
    radial_diff = diff_radial(centre_part)
    force_theta = (
        along_theta * theta_diff[:, 0]
        + along_phi * phi_diff[:, 3]
        + inv_spacing * radial_diff[:, 4]
        + curvature * (stress_tt - stress_pp)
        + 3.0 * inv_radius * stress_tr
    )
    force_phi = (
        along_theta * theta_diff[:, 3]
        + along_phi * phi_diff[:, 1]
        + inv_spacing * radial_diff[:, 5]
        + 2.0 * curvature * stress_tp
        + 3.0 * inv_radius * stress_pr
    )
    force_radial = (
        along_theta * theta_diff[:, 4]
        + along_phi * phi_diff[:, 5]
        + inv_spacing * radial_diff[:, 2]
        + inv_radius * (2.0 * stress_rr - stress_tt - stress_pp)
        + curvature * stress_tr
    )
    return jnp.stack([force_theta, force_phi, force_radial], 1)


def stress_rate(velocity, lame_field, shear_field, metric):
    along_theta, along_phi, curvature, inv_radius, inv_spacing = metric
    centre_part = velocity[..., 2:-2, 2:-2]
    vel_theta, vel_phi, vel_radial = (centre_part[:, 0], centre_part[:, 1], centre_part[:, 2])
    theta_diff = diff_theta(velocity)
    phi_diff = diff_phi(velocity)
    radial_diff = diff_radial(centre_part)
    strain_tt = along_theta * theta_diff[:, 0] + inv_radius * vel_radial
    strain_pp = along_phi * phi_diff[:, 1] + curvature * vel_theta + inv_radius * vel_radial
    strain_rr = inv_spacing * radial_diff[:, 2]
    strain_tp = 0.5 * (
        along_theta * theta_diff[:, 1] - curvature * vel_phi + along_phi * phi_diff[:, 0]
    )
    strain_tr = 0.5 * (
        inv_spacing * radial_diff[:, 0] - inv_radius * vel_theta + along_theta * theta_diff[:, 2]
    )
    strain_pr = 0.5 * (
        inv_spacing * radial_diff[:, 1] - inv_radius * vel_phi + along_phi * phi_diff[:, 2]
    )
    dilation = strain_tt + strain_pp + strain_rr
    double_shear = 2.0 * shear_field
    return jnp.stack(
        [
            lame_field * dilation + double_shear * strain_tt,
            lame_field * dilation + double_shear * strain_pp,
            lame_field * dilation + double_shear * strain_rr,
            double_shear * strain_tp,
            double_shear * strain_tr,
            double_shear * strain_pr,
        ],
        1,
    )


def lookup(layer_ids, values_table):
    looked = jnp.zeros(layer_ids.shape, jnp.float32)
    for layer_index in range(values_table.shape[0]):
        looked = looked + jnp.where(layer_ids == layer_index, values_table[layer_index], 0.0)
    return looked


def fold_pole(padded, rim_width, sign_flip):
    upper_strip = padded[..., rim_width : 2 * rim_width, :][..., ::-1, :] * sign_flip
    lower_strip = padded[..., -2 * rim_width : -rim_width, :][..., ::-1, :] * sign_flip
    arrived = from_behind(
        jnp.concatenate([upper_strip, lower_strip], -2), "lon", lax.axis_size("lon") // 2
    )
    band_index = lax.axis_index("colat")
    last_band = lax.axis_size("colat") - 1
    upper_rim = jnp.where(band_index == 0, arrived[..., :rim_width, :], padded[..., :rim_width, :])
    bottom = jnp.where(
        band_index == last_band, arrived[..., rim_width:, :], padded[..., -rim_width:, :]
    )
    return jnp.concatenate([upper_rim, padded[..., rim_width:-rim_width, :], bottom], -2)


def extend(fields, rim_width, sign_flip):
    wrapped = extended(fields, (("lon", 4),), rim_width, True)
    banded = extended(wrapped, (("colat", 3),), rim_width, False)
    return fold_pole(banded, rim_width, sign_flip)


def deposit(values, level_ids, row_ids, col_ids, levels, reach_rows, reach_cols):
    level_hot = (level_ids[:, None] == jnp.arange(levels, dtype=jnp.int32)[None, :]).astype(
        jnp.float32
    )
    row_hot = (row_ids[:, None] == jnp.arange(reach_rows, dtype=jnp.int32)[None, :]).astype(
        jnp.float32
    )
    col_hot = (col_ids[:, None] == jnp.arange(reach_cols, dtype=jnp.int32)[None, :]).astype(
        jnp.float32
    )
    weighted = (
        values[:, None, None, :]
        * jnp.transpose(level_hot)[None, :, None, :]
        * jnp.transpose(row_hot)[None, None, :, :]
    )
    count = values.shape[0]
    spread = jnp.dot(
        weighted.reshape(count * levels * reach_rows, -1),
        col_hot,
        precision=lax.Precision.HIGHEST,
        preferred_element_type=jnp.float32,
    )
    return spread.reshape(count, levels, reach_rows, reach_cols)


def inject(
    velocity,
    step_index,
    source_cells,
    source_wavelet,
    receiver_cells,
    receiver_residual,
    row_start,
    col_start,
    lat_cells,
    lon_cells,
):
    levels = velocity.shape[2]
    reach_rows = velocity.shape[-2]
    reach_cols = velocity.shape[-1]

    def locate(cell_ids):
        plane_cells = lat_cells * lon_cells
        level_ids = cell_ids // plane_cells
        row_ids = cell_ids % plane_cells // lon_cells - row_start
        col_ids = (cell_ids % lon_cells - col_start) % lon_cells
        return (level_ids, row_ids, col_ids)

    level_ids, row_ids, col_ids = locate(source_cells)
    source_part = deposit(
        source_wavelet[step_index][None, :],
        level_ids,
        row_ids,
        col_ids,
        levels,
        reach_rows,
        reach_cols,
    )
    level_ids, row_ids, col_ids = locate(receiver_cells)
    receiver_part = deposit(
        receiver_residual[step_index], level_ids, row_ids, col_ids, levels, reach_rows, reach_cols
    )
    forward_part = jnp.concatenate(
        [jnp.zeros((2,) + source_part.shape[1:], jnp.float32), source_part], 0
    )
    return velocity + jnp.stack([forward_part, receiver_part])


def on_device(
    forward_state,
    adjoint_state,
    layer_ids,
    density_table,
    lame_table,
    shear_table,
    source_cells,
    source_wavelet,
    receiver_cells,
    receiver_residual,
):
    levels, band_rows, tile_cols = layer_ids.shape
    lat_cells = band_rows * lax.axis_size("colat")
    lon_cells = tile_cols * lax.axis_size("lon")
    first_row = lax.axis_index("colat") * band_rows
    first_col = lax.axis_index("lon") * tile_cols
    step_size = time_step(lon_cells)
    inv_rho = 1.0 / lookup(layer_ids, density_table)
    lame_field = lookup(layer_ids, lame_table)
    shear_field = lookup(layer_ids, shear_table)
    vel_flip = jnp.array(VEL_SIGNS, dtype=jnp.float32)[:, None, None, None]
    stress_flip = jnp.array(STRESS_SIGNS, dtype=jnp.float32)[:, None, None, None]
    metric = geometry(
        first_row + jnp.arange(band_rows, dtype=jnp.int32), levels, lat_cells, lon_cells
    )
    stacked = jnp.stack([forward_state, adjoint_state])
    velocity = stacked[:, :3]
    stress = stacked[:, 3:]
    kernel = jnp.zeros(layer_ids.shape, jnp.float32)
    for step_index in range(STEPS):
        forcing = accelerate(extend(stress, 2, stress_flip), metric)
        velocity = velocity + step_size * inv_rho * forcing
        velocity = inject(
            velocity,
            step_index,
            source_cells,
            source_wavelet,
            receiver_cells,
            receiver_residual,
            first_row,
            first_col,
            lat_cells,
            lon_cells,
        )
        stress = stress + step_size * stress_rate(
            extend(velocity, 2, vel_flip), lame_field, shear_field, metric
        )
        kernel = kernel + jnp.sum(velocity[0] * velocity[1], 0)
    forward_field = jnp.concatenate([velocity[0], stress[0]], 0)
    adjoint_field = jnp.concatenate([velocity[1], stress[1]], 0)
    return (forward_field, adjoint_field, kernel)


def solution(mesh):
    return jax.shard_map(
        on_device,
        mesh=mesh,
        in_specs=(
            P(None, None, "colat", "lon"),
            P(None, None, "colat", "lon"),
            P(None, "colat", "lon"),
            P(),
            P(),
            P(),
            P(),
            P(),
            P(),
            P(),
        ),
        out_specs=(
            P(None, None, "colat", "lon"),
            P(None, None, "colat", "lon"),
            P(None, "colat", "lon"),
        ),
        check_vma=False,
    )
```

profile of v0, /device:TPU:8, one launch (start us, length us, event | category | flops | bytes accessed | tf_op | source)
XLA Modules:
  0.0 221.1 jit_solution(7928343728266530203)
XLA Ops:
  0.6 1.6 fusion.18
  2.9 17.9 %collective-permute-start.1 = (f32[2,6,8,16,2]{3,2,4,1,0:T(8,128)S(1)}, f32[2,6,8,16,2]{3,2,4,1,0:T(8,128)S(1)}, u32[]{:S(2)}, u32[]{:S(2)}) collective-permute-start(f32[2,6,8,16,2]{3,2,4,1,0:T(8,128)S(1)} %copy.16), channel_id=1, source_target_pairs={{32,0},{64,32},{96,64},{128,96},{160,128},{192,160},{224,192},{256... | collective-permute-start | bytes 36872 | tf_op jit(solution)/shard_map/ppermute | solution.py:32
  21.5 2.1 collective-permute-start
  25.4 10.8 %broadcast_multiply_fusion.8 = (f32[8,16,128]{2,1,0:T(8,128)}, f32[8,16,128]{2,1,0:T(8,128)S(1)}, pred[8,16,128]{2,1,0:T(8,128)(4,1)S(1)}, pred[8,16,128]{2,1,0:...) fusion(f32[]{:T(128)} %bitcast.56, f32[]{:T(128)} %bitcast.55, ...), kind=kLoop, calls=%fused_computation.319 | loop fusion | flops 786432 | bytes 458816 | tf_op jit(solution)/shard_map/mul | solution.py:132
  42.4 10.9 %divide_multiply_fusion = f32[8,16,128]{2,1,0:T(8,128)} fusion(pred[8,16,128]{2,1,0:T(8,128)(4,1)S(1)} %get-tuple-element.23, pred[8,16,128]{2,1,0:T(8,128)(4,1)S(1)} %get-tuple-element.22, pred[8,16,128]{2,1,0:T(8,128)(4,1)S(1)} %get-tuple-element.21, pred[8,16,128]{2,1,0:T(8,128)(4,1)S(1)} %get-tuple-element.20, ...), kind=kLoop, calls=%fused_computation.313 | loop fusion | flops 540672 | bytes 327744 | tf_op jit(solution)/shard_map/mul | solution.py:269
  53.3 10.7 %select_add_fusion.1 = f32[8,16,128]{2,1,0:T(8,128)} fusion(pred[8,16,128]{2,1,0:T(8,128)(4,1)S(1)} %get-tuple-element.23, pred[8,16,128]{2,1,0:T(8,128)(4,1)S(1)} %get-tuple-element.22, pred[8,16,128]{2,1,0:T(8,128)(4,1)S(1)} %get-tuple-element.21, pred[8,16,128]{2,1,0:T(8,128)(4,1)S(1)} %get-tuple-element.20, ...), kind=kLoop, calls=%fused_computation.312 | loop fusion | flops 507904 | bytes 327744 | tf_op jit(solution)/shard_map/add | solution.py:144
  65.3 1.5 copy.17
  66.8 1.4 pad_maximum_fusion.41
  68.3 1.9 rev.24
  70.2 1.9 rev.25
  72.1 1.3 broadcast_multiply_fusion.3
  73.6 2.2 %collective-permute-start.2 = (f32[2,6,8,4,132]{4,3,2,1,0:T(4,128)S(1)}, f32[2,6,8,4,132]{4,3,2,1,0:T(4,128)S(1)}, u32[]{:S(2)}, u32[]{:S(2)}) collective-permute-start(f32[2,6,8,4,132]{4,3,2,1,0:T(4,128)S(1)} %pad_maximum_fusion.34), channel_id=1, source_target_pairs={{0,512},{32,544},{64,576},{96,608},{128,640},{160,672},{192,704},{... | collective-permute-start | bytes 608264 | tf_op jit(solution)/shard_map/ppermute | solution.py:21
  75.9 6.8 %collective-permute-start.3 = (f32[2,6,8,2,132]{4,3,2,1,0:T(2,128)S(1)}, f32[2,6,8,2,132]{4,3,2,1,0:T(2,128)S(1)}, u32[]{:S(2)}, u32[]{:S(2)}) collective-permute-start(f32[2,6,8,2,132]{4,3,2,1,0:T(2,128)S(1)} %copy-done.19), channel_id=1, source_target_pairs={{1,0},{2,1},{3,2},{4,3},{5,4},{6,5},{7,6},{8,7},{9,8},{10,9},{11,1... | collective-permute-start | bytes 304136 | tf_op jit(solution)/shard_map/ppermute | solution.py:32
  82.8 1.9 collective-permute-start.4
  84.7 1.5 fusion.14
  86.2 9.8 %collective-permute-done.4 = f32[2,6,8,2,132]{4,3,2,1,0:T(2,128)S(1)} collective-permute-done((f32[2,6,8,2,132]{4,3,2,1,0:T(2,128)S(1)}, f32[2,6,8,2,132]{4,3,2,1,0:T(2,128)S(1)}, u32[]{:S(2)}, u32[]{:S(2)}) %collective-permute-start.4) | collective-permute-done | bytes 101408 | tf_op jit(solution)/shard_map/ppermute | solution.py:31
  99.6 6.4 %collective-permute-start.6 = (f32[2,3,8,16,2]{4,3,2,1,0:T(8,128)S(1)}, f32[2,3,8,16,2]{4,3,2,1,0:T(8,128)S(1)}, u32[]{:S(2)}, u32[]{:S(2)}) collective-permute-start(f32[2,3,8,16,2]{4,3,2,1,0:T(8,128)S(1)} %get-tuple-element.59), channel_id=1, source_target_pairs={{32,0},{64,32},{96,64},{128,96},{160,128},{192,160},{224,192},{256... | collective-permute-start | bytes 18440 | tf_op jit(solution)/shard_map/ppermute | solution.py:32
  106.0 1.9 collective-permute-start.5
  108.9 2.3 %collective-permute-done.6 = f32[2,3,8,16,2]{4,3,2,1,0:T(8,128)S(1)} collective-permute-done((f32[2,3,8,16,2]{4,3,2,1,0:T(8,128)S(1)}, f32[2,3,8,16,2]{4,3,2,1,0:T(8,128)S(1)}, u32[]{:S(2)}, u32[]{:S(2)}) %collective-permute-start.6) | collective-permute-done | bytes 6176 | tf_op jit(solution)/shard_map/ppermute | solution.py:32
  111.3 5.9 %collective-permute-done.5 = f32[2,3,8,16,2]{4,3,2,1,0:T(8,128)S(1)} collective-permute-done((f32[2,3,8,16,2]{4,3,2,1,0:T(8,128)S(1)}, f32[2,3,8,16,2]{4,3,2,1,0:T(8,128)S(1)}, u32[]{:S(2)}, u32[]{:S(2)}) %collective-permute-start.5) | collective-permute-done | bytes 6176 | tf_op jit(solution)/shard_map/ppermute | solution.py:31
  117.6 1.9 collective-permute-start.8
  120.2 4.8 %collective-permute-start.9 = (f32[2,3,8,2,132]{4,3,2,1,0:T(2,128)S(1)}, f32[2,3,8,2,132]{4,3,2,1,0:T(2,128)S(1)}, u32[]{:S(2)}, u32[]{:S(2)}) collective-permute-start(f32[2,3,8,2,132]{4,3,2,1,0:T(2,128)S(1)} %get-tuple-element.38), channel_id=1, source_target_pairs={{0,1},{1,2},{2,3},{3,4},{4,5},{5,6},{6,7},{7,8},{8,9},{9,10},{10,1... | collective-permute-start | bytes 152072 | tf_op jit(solution)/shard_map/ppermute | solution.py:31
  125.3 3.5 %collective-permute-start.7 = (f32[2,3,8,4,132]{4,3,2,1,0:T(4,128)S(1)}, f32[2,3,8,4,132]{4,3,2,1,0:T(4,128)S(1)}, u32[]{:S(2)}, u32[]{:S(2)}) collective-permute-start(f32[2,3,8,4,132]{4,3,2,1,0:T(4,128)S(1)} %pad_maximum_fusion.42), channel_id=1, source_target_pairs={{0,512},{32,544},{64,576},{96,608},{128,640},{160,672},{192,704},{... | collective-permute-start | bytes 304136 | tf_op jit(solution)/shard_map/ppermute | solution.py:21
  129.6 1.9 collective-permute-done.9
  136.4 2.4 %copy.22 = f32[2,6,8,16,2]{3,2,4,1,0:T(8,128)} copy(f32[2,6,8,16,2]{4,3,2,1,0:T(8,128)} %get-tuple-element.45) | data formatting | bytes 24576 | tf_op jit(solution)/shard_map/slice | solution.py:30
  138.8 2.5 %collective-permute-start.11 = (f32[2,6,8,16,2]{3,2,4,1,0:T(8,128)}, f32[2,6,8,16,2]{3,2,4,1,0:T(8,128)}, u32[]{:S(2)}, u32[]{:S(2)}) collective-permute-start(f32[2,6,8,16,2]{3,2,4,1,0:T(8,128)} %copy.22), channel_id=1, source_target_pairs={{32,0},{64,32},{96,64},{128,96},{160,128},{192,160},{224,192},{256... | collective-permute-start | bytes 36872 | tf_op jit(solution)/shard_map/ppermute | solution.py:32
  142.7 1.9 collective-permute-start.10
  144.6 1.5 pad_bitcast_fusion
  146.1 1.5 copy.24
  147.6 3.4 %collective-permute-done.10 = f32[2,6,8,16,2]{3,2,4,1,0:T(8,128)} collective-permute-done((f32[2,6,8,16,2]{3,2,4,1,0:T(8,128)}, f32[2,6,8,16,2]{3,2,4,1,0:T(8,128)}, u32[]{:S(2)}, u32[]{:S(2)}) %collective-permute-start.10) | collective-permute-done | bytes 12320 | tf_op jit(solution)/shard_map/ppermute | solution.py:31
  151.0 2.4 %copy.23 = f32[2,6,8,16,2]{4,3,2,1,0:T(8,128)} copy(f32[2,6,8,16,2]{3,2,4,1,0:T(8,128)} %collective-permute-done.10) | data formatting | bytes 24576 | tf_op jit(solution)/shard_map/ppermute | solution.py:31
  153.4 2.5 %pad_maximum_fusion.38 = (f32[2,6,8,2,132]{4,3,2,1,0:T(2,128)}, f32[2,6,8,2,132]{4,3,2,1,0:T(2,128)}) fusion(f32[2,6,8,16,2]{4,3,2,1,0:T(8,128)S(1)} %copy.24, f32[2,6,8,16,128]{4,3,2,1,0:T(8,128)S(1)} %multiply_add_fusion.1, f32[2,6,8,16,2]{4,3,2,1,0:T(8,128)} %copy.23), kind=kLoop, calls=%fused_computation.168 | loop fusion | flops 101376 | bytes 1013760 | tf_op jit(solution)/shard_map/slice | solution.py:149
  156.0 1.9 rev.28
  157.9 1.9 rev.29
  161.3 3.7 %collective-permute-start.12 = (f32[2,6,8,4,132]{4,3,2,1,0:T(4,128)S(1)}, f32[2,6,8,4,132]{4,3,2,1,0:T(4,128)S(1)}, u32[]{:S(2)}, u32[]{:S(2)}) collective-permute-start(f32[2,6,8,4,132]{4,3,2,1,0:T(4,128)S(1)} %pad_maximum_fusion.35), channel_id=1, source_target_pairs={{0,512},{32,544},{64,576},{96,608},{128,640},{160,672},{192,704},{... | collective-permute-start | bytes 608264 | tf_op jit(solution)/shard_map/ppermute | solution.py:21
  165.1 4.8 %collective-permute-start.13 = (f32[2,6,8,2,132]{4,3,2,1,0:T(2,128)S(1)}, f32[2,6,8,2,132]{4,3,2,1,0:T(2,128)S(1)}, u32[]{:S(2)}, u32[]{:S(2)}) collective-permute-start(f32[2,6,8,2,132]{4,3,2,1,0:T(2,128)S(1)} %copy-done.20), channel_id=1, source_target_pairs={{1,0},{2,1},{3,2},{4,3},{5,4},{6,5},{7,6},{8,7},{9,8},{10,9},{11,1... | collective-permute-start | bytes 304136 | tf_op jit(solution)/shard_map/ppermute | solution.py:32
  169.9 1.9 collective-permute-start.14
  171.9 1.5 fusion.8
  173.4 1.7 collective-permute-done.13
  175.0 7.5 %collective-permute-done.14 = f32[2,6,8,2,132]{4,3,2,1,0:T(2,128)S(1)} collective-permute-done((f32[2,6,8,2,132]{4,3,2,1,0:T(2,128)S(1)}, f32[2,6,8,2,132]{4,3,2,1,0:T(2,128)S(1)}, u32[]{:S(2)}, u32[]{:S(2)}) %collective-permute-start.14) | collective-permute-done | bytes 101408 | tf_op jit(solution)/shard_map/ppermute | solution.py:31
  186.3 3.1 %collective-permute-start.16 = (f32[2,3,8,16,2]{4,3,2,1,0:T(8,128)S(1)}, f32[2,3,8,16,2]{4,3,2,1,0:T(8,128)S(1)}, u32[]{:S(2)}, u32[]{:S(2)}) collective-permute-start(f32[2,3,8,16,2]{4,3,2,1,0:T(8,128)S(1)} %get-tuple-element.53), channel_id=1, source_target_pairs={{32,0},{64,32},{96,64},{128,96},{160,128},{192,160},{224,192},{256... | collective-permute-start | bytes 18440 | tf_op jit(solution)/shard_map/ppermute | solution.py:32
  189.4 1.9 collective-permute-start.15
  192.0 2.7 %collective-permute-done.16 = f32[2,3,8,16,2]{4,3,2,1,0:T(8,128)S(1)} collective-permute-done((f32[2,3,8,16,2]{4,3,2,1,0:T(8,128)S(1)}, f32[2,3,8,16,2]{4,3,2,1,0:T(8,128)S(1)}, u32[]{:S(2)}, u32[]{:S(2)}) %collective-permute-start.16) | collective-permute-done | bytes 6176 | tf_op jit(solution)/shard_map/ppermute | solution.py:32
  194.7 5.9 %collective-permute-done.15 = f32[2,3,8,16,2]{4,3,2,1,0:T(8,128)S(1)} collective-permute-done((f32[2,3,8,16,2]{4,3,2,1,0:T(8,128)S(1)}, f32[2,3,8,16,2]{4,3,2,1,0:T(8,128)S(1)}, u32[]{:S(2)}, u32[]{:S(2)}) %collective-permute-start.15) | collective-permute-done | bytes 6176 | tf_op jit(solution)/shard_map/ppermute | solution.py:31
  201.0 1.9 collective-permute-start.18
  203.6 4.8 %collective-permute-start.19 = (f32[2,3,8,2,132]{4,3,2,1,0:T(2,128)S(1)}, f32[2,3,8,2,132]{4,3,2,1,0:T(2,128)S(1)}, u32[]{:S(2)}, u32[]{:S(2)}) collective-permute-start(f32[2,3,8,2,132]{4,3,2,1,0:T(2,128)S(1)} %get-tuple-element.36), channel_id=1, source_target_pairs={{0,1},{1,2},{2,3},{3,4},{4,5},{5,6},{6,7},{7,8},{8,9},{9,10},{10,1... | collective-permute-start | bytes 152072 | tf_op jit(solution)/shard_map/ppermute | solution.py:31
  208.7 3.2 %collective-permute-start.17 = (f32[2,3,8,4,132]{4,3,2,1,0:T(4,128)S(1)}, f32[2,3,8,4,132]{4,3,2,1,0:T(4,128)S(1)}, u32[]{:S(2)}, u32[]{:S(2)}) collective-permute-start(f32[2,3,8,4,132]{4,3,2,1,0:T(4,128)S(1)} %pad_maximum_fusion.43), channel_id=1, source_target_pairs={{0,512},{32,544},{64,576},{96,608},{128,640},{160,672},{192,704},{... | collective-permute-start | bytes 304136 | tf_op jit(solution)/shard_map/ppermute | solution.py:21
  212.6 2.5 %collective-permute-done.19 = f32[2,3,8,2,132]{4,3,2,1,0:T(2,128)S(1)} collective-permute-done((f32[2,3,8,2,132]{4,3,2,1,0:T(2,128)S(1)}, f32[2,3,8,2,132]{4,3,2,1,0:T(2,128)S(1)}, u32[]{:S(2)}, u32[]{:S(2)}) %collective-permute-start.19) | collective-permute-done | bytes 50720 | tf_op jit(solution)/shard_map/ppermute | solution.py:31
  (183 shorter events, 37.1 us)
Async XLA Ops:
  2.3 21.3 %copy-start = (f32[9,8,16,128]{3,2,1,0:T(8,128)S(1)}, f32[9,8,16,128]{3,2,1,0:T(8,128)}, u32[]{:S(2)}) copy-start(f32[9,8,16,128]{3,2,1,0:T(8,128)} %param.12) | copy-start | bytes 1769476
  2.3 21.3 %copy-start.1 = (f32[9,8,16,128]{3,2,1,0:T(8,128)S(1)}, f32[9,8,16,128]{3,2,1,0:T(8,128)}, u32[]{:S(2)}) copy-start(f32[9,8,16,128]{3,2,1,0:T(8,128)} %param.13) | copy-start | bytes 1769476
  2.9 61.8 %collective-permute-start.1 = (f32[2,6,8,16,2]{3,2,4,1,0:T(8,128)S(1)}, f32[2,6,8,16,2]{3,2,4,1,0:T(8,128)S(1)}, u32[]{:S(2)}, u32[]{:S(2)}) collective-permute-start(f32[2,6,8,16,2]{3,2,4,1,0:T(8,128)S(1)} %copy.16), channel_id=1, source_target_pairs={{32,0},{64,32},{96,64},{128,96},{160,128},{192,160},{224,192},{256... | collective-permute-start | bytes 36872 | tf_op jit(solution)/shard_map/ppermute | solution.py:32
  21.4 2.3 %copy-start.40 = (s32[512]{0:T(512)S(1)}, s32[512]{0:T(512)}, u32[]{:S(2)}) copy-start(s32[512]{0:T(512)} %param.20) | copy-start | bytes 6148
  21.4 2.4 %copy-start.32 = (f32[2,3,512]{2,0,1:T(2,128)S(1)}, f32[2,3,512]{2,0,1:T(2,128)}, u32[]{:S(2)}) copy-start(f32[2,3,512]{2,0,1:T(2,128)} %param.21) | copy-start | bytes 36868
  21.5 2.4 %copy-start.43 = (s32[8]{0:T(128)S(1)}, s32[8]{0:T(128)}, u32[]{:S(2)}) copy-start(s32[8]{0:T(128)} %param.18) | copy-start | bytes 100
  21.5 2.5 %copy-start.42 = (f32[2,8]{1,0:T(2,128)S(1)}, f32[2,8]{1,0:T(2,128)}, u32[]{:S(2)}) copy-start(f32[2,8]{1,0:T(2,128)} %param.19) | copy-start | bytes 196
  21.5 2.5 %copy-start.26 = (f32[16]{0:T(128)S(1)}, f32[16]{0:T(128)}, u32[]{:S(2)}) copy-start(f32[16]{0:T(128)} %param.17) | copy-start | bytes 196
  21.5 3.2 %copy-start.27 = (f32[16]{0:T(128)S(1)}, f32[16]{0:T(128)}, u32[]{:S(2)}) copy-start(f32[16]{0:T(128)} %param.15) | copy-start | bytes 196
  21.5 3.9 %copy-start.29 = (s32[8,16,128]{2,1,0:T(8,128)S(1)}, s32[8,16,128]{2,1,0:T(8,128)}, u32[]{:S(2)}) copy-start(s32[8,16,128]{2,1,0:T(8,128)} %param.14) | copy-start | bytes 196612
  21.5 43.8 %collective-permute-start = (f32[2,6,8,16,2]{3,2,4,1,0:T(8,128)S(1)}, f32[2,6,8,16,2]{3,2,4,1,0:T(8,128)}, u32[]{:S(2)}, u32[]{:S(2)}) collective-permute-start(f32[2,6,8,16,2]{3,2,4,1,0:T(8,128)S(1)} %copy.15), channel_id=1, source_target_pairs={{0,32},{32,64},{64,96},{96,128},{128,160},{160,192},{192,224},{224... | collective-permute-start | bytes 36872 | tf_op jit(solution)/shard_map/ppermute | solution.py:31
  23.7 13.9 %copy-start.28 = (f32[16]{0:T(128)S(1)}, f32[16]{0:T(128)}, u32[]{:S(2)}) copy-start(f32[16]{0:T(128)} %param.16) | copy-start | bytes 196
  23.9 18.2 %copy-start.44 = (s32[8]{0:T(128)}, s32[8]{0:T(128)S(1)}, u32[]{:S(2)}) copy-start(s32[8]{0:T(128)S(1)} %get-tuple-element.134) | copy-start | bytes 100
  24.0 18.1 %copy-start.35 = (f32[16,8]{0,1:T(8,128)}, f32[16,8]{0,1:T(8,128)S(1)}, u32[]{:S(2)}) copy-start(f32[16,8]{0,1:T(8,128)S(1)} %fusion.150) | copy-start | bytes 1540
  68.3 3.8 %copy-start.41 = (f32[6]{0:T(128)S(1)}, f32[6]{0:T(128)}, u32[]{:S(2)}) copy-start(f32[6]{0:T(128)} %constant.223.clone) | copy-start | bytes 76
  72.1 3.8 %copy-start.19 = (f32[2,6,8,2,132]{4,3,2,1,0:T(2,128)S(1)}, f32[2,6,8,2,132]{4,3,2,1,0:T(2,128)}, u32[]{:S(2)}) copy-start(f32[2,6,8,2,132]{4,3,2,1,0:T(2,128)} %get-tuple-element.33) | copy-start | bytes 304132
  72.1 10.7 %copy-start.17 = (f32[2,6,8,2,132]{4,3,2,1,0:T(2,128)S(1)}, f32[2,6,8,2,132]{4,3,2,1,0:T(2,128)}, u32[]{:S(2)}) copy-start(f32[2,6,8,2,132]{4,3,2,1,0:T(2,128)} %get-tuple-element.34) | copy-start | bytes 304132
  73.6 22.3 %collective-permute-start.2 = (f32[2,6,8,4,132]{4,3,2,1,0:T(4,128)S(1)}, f32[2,6,8,4,132]{4,3,2,1,0:T(4,128)S(1)}, u32[]{:S(2)}, u32[]{:S(2)}) collective-permute-start(f32[2,6,8,4,132]{4,3,2,1,0:T(4,128)S(1)} %pad_maximum_fusion.34), channel_id=1, source_target_pairs={{0,512},{32,544},{64,576},{96,608},{128,640},{160,672},{192,704},{... | collective-permute-start | bytes 608264 | tf_op jit(solution)/shard_map/ppermute | solution.py:21
  75.9 21.8 %copy-start.33 = (f32[8]{0:T(128)}, f32[8]{0:T(128)S(1)}, u32[]{:S(2)}) copy-start(f32[8]{0:T(128)S(1)} %get-tuple-element.142) | copy-start | bytes 100
  75.9 10.3 %collective-permute-start.3 = (f32[2,6,8,2,132]{4,3,2,1,0:T(2,128)S(1)}, f32[2,6,8,2,132]{4,3,2,1,0:T(2,128)S(1)}, u32[]{:S(2)}, u32[]{:S(2)}) collective-permute-start(f32[2,6,8,2,132]{4,3,2,1,0:T(2,128)S(1)} %copy-done.19), channel_id=1, source_target_pairs={{1,0},{2,1},{3,2},{4,3},{5,4},{6,5},{7,6},{8,7},{9,8},{10,9},{11,1... | collective-permute-start | bytes 304136 | tf_op jit(solution)/shard_map/ppermute | solution.py:32
  82.8 13.2 %collective-permute-start.4 = (f32[2,6,8,2,132]{4,3,2,1,0:T(2,128)S(1)}, f32[2,6,8,2,132]{4,3,2,1,0:T(2,128)S(1)}, u32[]{:S(2)}, u32[]{:S(2)}) collective-permute-start(f32[2,6,8,2,132]{4,3,2,1,0:T(2,128)S(1)} %copy-done.17), channel_id=1, source_target_pairs={{0,1},{1,2},{2,3},{3,4},{4,5},{5,6},{6,7},{7,8},{8,9},{9,10},{10,1... | collective-permute-start | bytes 304136 | tf_op jit(solution)/shard_map/ppermute | solution.py:31
  98.2 1.1 copy-start.23
  99.4 8.5 %copy-start.36 = (f32[16,8]{0,1:T(8,128)S(1)}, f32[16,8]{0,1:T(8,128)}, u32[]{:S(2)}) copy-start(f32[16,8]{0,1:T(8,128)} %copy-done.35) | copy-start | bytes 1540
  99.4 8.5 %copy-start.37 = (f32[8,8]{1,0:T(8,128)S(1)}, f32[8,8]{1,0:T(8,128)}, u32[]{:S(2)}) copy-start(f32[8,8]{1,0:T(8,128)} %get-tuple-element.80) | copy-start | bytes 772
  99.4 8.5 %copy-start.45 = (s32[8]{0:T(128)S(1)}, s32[8]{0:T(128)}, u32[]{:S(2)}) copy-start(s32[8]{0:T(128)} %copy-done.44) | copy-start | bytes 100
  99.6 11.7 %collective-permute-start.6 = (f32[2,3,8,16,2]{4,3,2,1,0:T(8,128)S(1)}, f32[2,3,8,16,2]{4,3,2,1,0:T(8,128)S(1)}, u32[]{:S(2)}, u32[]{:S(2)}) collective-permute-start(f32[2,3,8,16,2]{4,3,2,1,0:T(8,128)S(1)} %get-tuple-element.59), channel_id=1, source_target_pairs={{32,0},{64,32},{96,64},{128,96},{160,128},{192,160},{224,192},{256... | collective-permute-start | bytes 18440 | tf_op jit(solution)/shard_map/ppermute | solution.py:32
  106.0 11.2 %collective-permute-start.5 = (f32[2,3,8,16,2]{4,3,2,1,0:T(8,128)S(1)}, f32[2,3,8,16,2]{4,3,2,1,0:T(8,128)S(1)}, u32[]{:S(2)}, u32[]{:S(2)}) collective-permute-start(f32[2,3,8,16,2]{4,3,2,1,0:T(8,128)S(1)} %get-tuple-element.60), channel_id=1, source_target_pairs={{0,32},{32,64},{64,96},{96,128},{128,160},{160,192},{192,224},{224... | collective-permute-start | bytes 18440 | tf_op jit(solution)/shard_map/ppermute | solution.py:31
  111.3 13.7 %copy-start.38 = (f32[3]{0:T(128)S(1)}, f32[3]{0:T(128)}, u32[]{:S(2)}) copy-start(f32[3]{0:T(128)} %constant.222.clone) | copy-start | bytes 40
  117.6 12.0 %collective-permute-start.8 = (f32[2,3,8,2,132]{4,3,2,1,0:T(2,128)S(1)}, f32[2,3,8,2,132]{4,3,2,1,0:T(2,128)S(1)}, u32[]{:S(2)}, u32[]{:S(2)}) collective-permute-start(f32[2,3,8,2,132]{4,3,2,1,0:T(2,128)S(1)} %get-tuple-element.37), channel_id=1, source_target_pairs={{1,0},{2,1},{3,2},{4,3},{5,4},{6,5},{7,6},{8,7},{9,8},{10,9},{11,1... | collective-permute-start | bytes 152072 | tf_op jit(solution)/shard_map/ppermute | solution.py:32
  120.2 11.4 %collective-permute-start.9 = (f32[2,3,8,2,132]{4,3,2,1,0:T(2,128)S(1)}, f32[2,3,8,2,132]{4,3,2,1,0:T(2,128)S(1)}, u32[]{:S(2)}, u32[]{:S(2)}) collective-permute-start(f32[2,3,8,2,132]{4,3,2,1,0:T(2,128)S(1)} %get-tuple-element.38), channel_id=1, source_target_pairs={{0,1},{1,2},{2,3},{3,4},{4,5},{5,6},{6,7},{7,8},{8,9},{9,10},{10,1... | collective-permute-start | bytes 152072 | tf_op jit(solution)/shard_map/ppermute | solution.py:31
  125.3 7.6 %collective-permute-start.7 = (f32[2,3,8,4,132]{4,3,2,1,0:T(4,128)S(1)}, f32[2,3,8,4,132]{4,3,2,1,0:T(4,128)S(1)}, u32[]{:S(2)}, u32[]{:S(2)}) collective-permute-start(f32[2,3,8,4,132]{4,3,2,1,0:T(4,128)S(1)} %pad_maximum_fusion.42), channel_id=1, source_target_pairs={{0,512},{32,544},{64,576},{96,608},{128,640},{160,672},{192,704},{... | collective-permute-start | bytes 304136 | tf_op jit(solution)/shard_map/ppermute | solution.py:21
  138.8 7.3 %collective-permute-start.11 = (f32[2,6,8,16,2]{3,2,4,1,0:T(8,128)}, f32[2,6,8,16,2]{3,2,4,1,0:T(8,128)}, u32[]{:S(2)}, u32[]{:S(2)}) collective-permute-start(f32[2,6,8,16,2]{3,2,4,1,0:T(8,128)} %copy.22), channel_id=1, source_target_pairs={{32,0},{64,32},{96,64},{128,96},{160,128},{192,160},{224,192},{256... | collective-permute-start | bytes 36872 | tf_op jit(solution)/shard_map/ppermute | solution.py:32
  142.7 8.4 %collective-permute-start.10 = (f32[2,6,8,16,2]{3,2,4,1,0:T(8,128)}, f32[2,6,8,16,2]{3,2,4,1,0:T(8,128)}, u32[]{:S(2)}, u32[]{:S(2)}) collective-permute-start(f32[2,6,8,16,2]{3,2,4,1,0:T(8,128)} %copy.21), channel_id=1, source_target_pairs={{0,32},{32,64},{64,96},{96,128},{128,160},{160,192},{192,224},{224... | collective-permute-start | bytes 36872 | tf_op jit(solution)/shard_map/ppermute | solution.py:31
  161.1 4.0 %copy-start.20 = (f32[2,6,8,2,132]{4,3,2,1,0:T(2,128)S(1)}, f32[2,6,8,2,132]{4,3,2,1,0:T(2,128)}, u32[]{:S(2)}) copy-start(f32[2,6,8,2,132]{4,3,2,1,0:T(2,128)} %get-tuple-element.31) | copy-start | bytes 304132
  161.1 8.8 %copy-start.18 = (f32[2,6,8,2,132]{4,3,2,1,0:T(2,128)S(1)}, f32[2,6,8,2,132]{4,3,2,1,0:T(2,128)}, u32[]{:S(2)}) copy-start(f32[2,6,8,2,132]{4,3,2,1,0:T(2,128)} %get-tuple-element.32) | copy-start | bytes 304132
  161.1 10.7 %copy-start.2 = (f32[2,6,8,16,2]{4,3,2,1,0:T(8,128)S(1)}, f32[2,6,8,16,2]{4,3,2,1,0:T(8,128)}, u32[]{:S(2)}) copy-start(f32[2,6,8,16,2]{4,3,2,1,0:T(8,128)} %copy.23) | copy-start | bytes 36868
  161.3 21.2 %collective-permute-start.12 = (f32[2,6,8,4,132]{4,3,2,1,0:T(4,128)S(1)}, f32[2,6,8,4,132]{4,3,2,1,0:T(4,128)S(1)}, u32[]{:S(2)}, u32[]{:S(2)}) collective-permute-start(f32[2,6,8,4,132]{4,3,2,1,0:T(4,128)S(1)} %pad_maximum_fusion.35), channel_id=1, source_target_pairs={{0,512},{32,544},{64,576},{96,608},{128,640},{160,672},{192,704},{... | collective-permute-start | bytes 608264 | tf_op jit(solution)/shard_map/ppermute | solution.py:21
  165.1 10.0 %collective-permute-start.13 = (f32[2,6,8,2,132]{4,3,2,1,0:T(2,128)S(1)}, f32[2,6,8,2,132]{4,3,2,1,0:T(2,128)S(1)}, u32[]{:S(2)}, u32[]{:S(2)}) collective-permute-start(f32[2,6,8,2,132]{4,3,2,1,0:T(2,128)S(1)} %copy-done.20), channel_id=1, source_target_pairs={{1,0},{2,1},{3,2},{4,3},{5,4},{6,5},{7,6},{8,7},{9,8},{10,9},{11,1... | collective-permute-start | bytes 304136 | tf_op jit(solution)/shard_map/ppermute | solution.py:32
  169.9 12.6 %collective-permute-start.14 = (f32[2,6,8,2,132]{4,3,2,1,0:T(2,128)S(1)}, f32[2,6,8,2,132]{4,3,2,1,0:T(2,128)S(1)}, u32[]{:S(2)}, u32[]{:S(2)}) collective-permute-start(f32[2,6,8,2,132]{4,3,2,1,0:T(2,128)S(1)} %copy-done.18), channel_id=1, source_target_pairs={{0,1},{1,2},{2,3},{3,4},{4,5},{5,6},{6,7},{7,8},{8,9},{9,10},{10,1... | collective-permute-start | bytes 304136 | tf_op jit(solution)/shard_map/ppermute | solution.py:31
  182.8 1.3 copy-start.34
  184.8 1.1 copy-start.15
  184.8 1.2 copy-start.16
  186.3 8.4 %collective-permute-start.16 = (f32[2,3,8,16,2]{4,3,2,1,0:T(8,128)S(1)}, f32[2,3,8,16,2]{4,3,2,1,0:T(8,128)S(1)}, u32[]{:S(2)}, u32[]{:S(2)}) collective-permute-start(f32[2,3,8,16,2]{4,3,2,1,0:T(8,128)S(1)} %get-tuple-element.53), channel_id=1, source_target_pairs={{32,0},{64,32},{96,64},{128,96},{160,128},{192,160},{224,192},{256... | collective-permute-start | bytes 18440 | tf_op jit(solution)/shard_map/ppermute | solution.py:32
  189.4 11.2 %collective-permute-start.15 = (f32[2,3,8,16,2]{4,3,2,1,0:T(8,128)S(1)}, f32[2,3,8,16,2]{4,3,2,1,0:T(8,128)S(1)}, u32[]{:S(2)}, u32[]{:S(2)}) collective-permute-start(f32[2,3,8,16,2]{4,3,2,1,0:T(8,128)S(1)} %get-tuple-element.54), channel_id=1, source_target_pairs={{0,32},{32,64},{64,96},{96,128},{128,160},{160,192},{192,224},{224... | collective-permute-start | bytes 18440 | tf_op jit(solution)/shard_map/ppermute | solution.py:31
  194.7 13.7 %copy-start.39 = (f32[3]{0:T(128)S(1)}, f32[3]{0:T(128)}, u32[]{:S(2)}) copy-start(f32[3]{0:T(128)} %constant.222.clone) | copy-start | bytes 40
  201.0 11.6 %collective-permute-start.18 = (f32[2,3,8,2,132]{4,3,2,1,0:T(2,128)S(1)}, f32[2,3,8,2,132]{4,3,2,1,0:T(2,128)}, u32[]{:S(2)}, u32[]{:S(2)}) collective-permute-start(f32[2,3,8,2,132]{4,3,2,1,0:T(2,128)S(1)} %get-tuple-element.35), channel_id=1, source_target_pairs={{1,0},{2,1},{3,2},{4,3},{5,4},{6,5},{7,6},{8,7},{9,8},{10,9},{11,1... | collective-permute-start | bytes 152072 | tf_op jit(solution)/shard_map/ppermute | solution.py:32
  203.6 11.6 %collective-permute-start.19 = (f32[2,3,8,2,132]{4,3,2,1,0:T(2,128)S(1)}, f32[2,3,8,2,132]{4,3,2,1,0:T(2,128)S(1)}, u32[]{:S(2)}, u32[]{:S(2)}) collective-permute-start(f32[2,3,8,2,132]{4,3,2,1,0:T(2,128)S(1)} %get-tuple-element.36), channel_id=1, source_target_pairs={{0,1},{1,2},{2,3},{3,4},{4,5},{5,6},{6,7},{7,8},{8,9},{9,10},{10,1... | collective-permute-start | bytes 152072 | tf_op jit(solution)/shard_map/ppermute | solution.py:31
  208.7 7.6 %collective-permute-start.17 = (f32[2,3,8,4,132]{4,3,2,1,0:T(4,128)S(1)}, f32[2,3,8,4,132]{4,3,2,1,0:T(4,128)S(1)}, u32[]{:S(2)}, u32[]{:S(2)}) collective-permute-start(f32[2,3,8,4,132]{4,3,2,1,0:T(4,128)S(1)} %pad_maximum_fusion.43), channel_id=1, source_target_pairs={{0,512},{32,544},{64,576},{96,608},{128,640},{160,672},{192,704},{... | collective-permute-start | bytes 304136 | tf_op jit(solution)/shard_map/ppermute | solution.py:21
  (18 other events, 15.4 us)
where the time goes:
time: 223 us; the launch traced here: 221 us
  starting transfers between devices  79.3 us (36%)
  other arithmetic  59 us (26%)
  waiting for transfers between devices  46 us (21%)
  local copies, waits for them, and re-layouts  31.1 us (14%)
  matrix products  3.89 us (2%)
    ppermute x8, starting transfers between devices, extended(): after = lax.ppermute(leading, axis, down)  45.4 us
    ppermute x8, waiting for transfers between devices, extended(): before = lax.ppermute(last, axis, up)  36.9 us
    ppermute x8, starting transfers between devices, extended(): before = lax.ppermute(last, axis, up)  21.3 us
    ppermute x4, starting transfers between devices, from_behind(): return lax.ppermute(value, axis, pairs)  12.6 us
    mul x1, other arithmetic, on_device(): velocity = velocity + step_size * inv_rho * forcing  10.9 us
    mul x1, other arithmetic, stress_rate(): double_shear * strain_rr  10.8 us
    add x1, other arithmetic, lookup(): looked + jnp.where(layer_ids == layer_index, values_table[layer_index], 0.0)  10.7 us
    ppermute x8, waiting for transfers between devices, extended(): after = lax.ppermute(leading, axis, down)  6.71 us
  transfers between devices with their start and end apart: 20, of which 12 were waited for; matrix products, arithmetic and copies ran while one was open for 24% of the time, Pallas kernels for 0%

commit v1 on v0

v1 whole, which is shorter than its diff:
```python
import functools
import math

import jax
import jax.numpy as jnp
from jax import lax
from jax.experimental import pallas as pl
from jax.experimental.pallas import tpu as pltpu
from jax.sharding import PartitionSpec as P

STEPS = 2
R_INNER = 0.55
COURANT = 0.3
SIN_FLOOR = 0.25
MESH = pl.DeviceIdType.MESH
F32 = jnp.float32

LEV, ROWS, LANES = 8, 16, 128
TT, TR, TP, PP, PR, RR = range(6)
STATE_OF = (3, 7, 6, 4, 8, 5)
CHUNK = 4


def lane_roll(x, shift):
    return pltpu.roll(x, shift % LANES, x.ndim - 1)


def kernel(
    n_lon,
    n_lat,
    fwd_hbm,
    adj_hbm,
    ids_hbm,
    density_ref,
    lame_ref,
    shear_ref,
    src_ref,
    wave_ref,
    cells_ref,
    resid_ref,
    fwd_out,
    adj_out,
    kern_out,
    state_in,
    ids_in,
    state_o,
    kern_o,
    stress,
    vel,
    part_v,
    part_s,
    inject,
    source,
    coef,
    col_recv,
    lon_send,
    lon_recv,
    in_sem,
    out_sem,
    col_ssem,
    col_rsem,
    lon_ssem,
    lon_rsem,
):
    lon = lax.axis_index("lon")
    lat = lax.axis_index("colat")
    lat_cells, lon_cells = n_lat * ROWS, n_lon * LANES
    is_top = 1 - lax.div(lat + n_lat - 1, n_lat)
    is_bot = lax.div(lat + 1, n_lat)
    left = lax.rem(lon + n_lon - 1, n_lon)
    right = lax.rem(lon + 1, n_lon)
    up = {
        "lon": lax.rem(lon + is_top * (n_lon // 2), n_lon),
        "colat": lat - 1 + is_top,
    }
    down = {
        "lon": lax.rem(lon + is_bot * (n_lon // 2), n_lon),
        "colat": lat + 1 - is_bot,
    }
    to_left = {"lon": left, "colat": lat}
    to_right = {"lon": right, "colat": lat}

    barrier = pltpu.get_barrier_semaphore()
    for peer in (up, down, to_left, to_right):
        pl.semaphore_signal(barrier, inc=1, device_id=peer, device_id_type=MESH)

    loads = [
        pltpu.make_async_copy(fwd_hbm, state_in.at[0], in_sem.at[0]),
        pltpu.make_async_copy(adj_hbm, state_in.at[1], in_sem.at[1]),
        pltpu.make_async_copy(ids_hbm, ids_in, in_sem.at[2]),
    ]
    for load in loads:
        load.start()

    theta_step = math.pi / lat_cells
    phi_step = 2.0 * math.pi / lon_cells
    delta_r = (1.0 - R_INNER) / LEV
    step_size = COURANT * SIN_FLOOR * R_INNER * phi_step / 1.6
    level = lax.broadcasted_iota(jnp.int32, (LEV, LANES), 0)
    lane = lax.broadcasted_iota(jnp.int32, (LEV, LANES), 1)
    ir = 1.0 / (R_INNER + (level.astype(F32) + 0.5) * delta_r)
    at = ir * (1.0 / (12.0 * theta_step))
    c_up = jnp.where(level < LEV - 1, 0.5 / delta_r, 0.0).astype(F32)
    c_dn = jnp.where(level > 0, 0.5 / delta_r, 0.0).astype(F32)

    rows3 = lax.broadcasted_iota(jnp.int32, (ROWS, LEV, LANES), 0) + lat * ROWS
    theta = (rows3.astype(F32) + 0.5) * theta_step
    sines = jnp.maximum(jnp.sin(theta), SIN_FLOOR)
    coef[0] = ir[None] / (sines * (12.0 * phi_step))
    coef[1] = jnp.cos(theta) / sines * ir[None]

    for step in range(STEPS):
        for f in range(2):
            zero = jnp.zeros((3, 2, LEV, LANES), F32)
            stress[step, f, 0:3, 0:2] = zero
            stress[step, f, 0:3, ROWS + 2 : ROWS + 4] = zero
            vel[step, f, :, 0:2] = zero
            vel[step, f, :, ROWS + 2 : ROWS + 4] = zero

    def unpack_state(f):
        for c in range(6):
            for row in range(ROWS):
                start = STATE_OF[c] * (LEV * ROWS) + row
                stress[0, f, c, 2 + row] = state_in[f, pl.ds(start, LEV, stride=ROWS), :]

    def send_cols(phase, f, ref):
        dst_slot = 1 - is_top
        a = pltpu.make_async_remote_copy(
            src_ref=ref.at[0:3, 2:4],
            dst_ref=col_recv.at[phase, f, dst_slot],
            send_sem=col_ssem.at[phase, f, 0],
            recv_sem=col_rsem.at[phase, f, dst_slot],
            device_id=up,
            device_id_type=MESH,
        )
        b = pltpu.make_async_remote_copy(
            src_ref=ref.at[0:3, ROWS : ROWS + 2],
            dst_ref=col_recv.at[phase, f, is_bot],
            send_sem=col_ssem.at[phase, f, 1],
            recv_sem=col_rsem.at[phase, f, is_bot],
            device_id=down,
            device_id_type=MESH,
        )
        a.start()
        b.start()
        return [a, b]

    quad = lax.div(lane, 4)
    spot = lax.rem(lane, 4)

    def pack_rim(rows_of):
        packed = []
        for group in range(2):
            acc = jnp.zeros((LEV, LANES), F32)
            for slot in range(32):
                k = group * 32 + slot
                if k < 48:
                    acc = jnp.where(quad == slot, lane_roll(rows_of(k // ROWS, k % ROWS), 4 * slot + 2), acc)
            packed.append(acc)
        return packed

    def send_lons(phase, f, rows_of):
        packed = pack_rim(rows_of)
        for group in range(2):
            lon_send[phase, f, group] = packed[group]
        copies = []
        for slot, peer in ((0, to_right), (1, to_left)):
            copy = pltpu.make_async_remote_copy(
                src_ref=lon_send.at[phase, f],
                dst_ref=lon_recv.at[phase, f, slot],
                send_sem=lon_ssem.at[phase, f, slot],
                recv_sem=lon_rsem.at[phase, f, slot],
                device_id=peer,
                device_id_type=MESH,
            )
            copy.start()
            copies.append(copy)
        return copies

    def wait_halo(phase, f):
        for slot in range(2):
            pltpu.make_async_remote_copy(
                src_ref=col_recv.at[phase, f, slot],
                dst_ref=col_recv.at[phase, f, slot],
                send_sem=col_ssem.at[phase, f, slot],
                recv_sem=col_rsem.at[phase, f, slot],
                device_id=up,
                device_id_type=MESH,
            ).wait_recv()
            pltpu.make_async_remote_copy(
                src_ref=lon_send.at[phase, f],
                dst_ref=lon_recv.at[phase, f, slot],
                send_sem=lon_ssem.at[phase, f, slot],
                recv_sem=lon_rsem.at[phase, f, slot],
                device_id=to_left,
                device_id_type=MESH,
            ).wait_recv()

    def rim_terms(phase, f):
        out = []
        for group in range(2):
            own = lon_send[phase, f, group]
            halo = jnp.where(spot < 2, lon_recv[phase, f, 0, group], lon_recv[phase, f, 1, group]) - own
            next1, next2 = lane_roll(halo, -1), lane_roll(halo, -2)
            prev1, prev2 = lane_roll(halo, 1), lane_roll(halo, 2)
            term = jnp.where(
                spot == 0,
                -next2,
                jnp.where(spot == 1, 8.0 * next1 - next2, jnp.where(spot == 2, prev2 - 8.0 * prev1, prev2)),
            )
            out.append(term)
        return out

    edge = (lane < 2) | (lane >= LANES - 2)

    def rim_of(terms, c, row):
        k = c * ROWS + row
        return jnp.where(edge, lane_roll(terms[k // 32], -(4 * (k % 32) + 2)), 0.0)

    def band_terms(phase, f, signs):
        flip_top = 1.0 - 2.0 * is_top.astype(F32)
        flip_bot = 1.0 - 2.0 * is_bot.astype(F32)
        terms = {}
        for c in range(3):
            near_top = col_recv[phase, f, 0, c, 1 - is_top]
            far_top = col_recv[phase, f, 0, c, is_top]
            near_bot = col_recv[phase, f, 1, c, is_bot]
            far_bot = col_recv[phase, f, 1, c, 1 - is_bot]
            if signs[c] < 0:
                near_top, far_top = near_top * flip_top, far_top * flip_top
                near_bot, far_bot = near_bot * flip_bot, far_bot * flip_bot
            terms[c, 0] = far_top - 8.0 * near_top
            terms[c, 1] = near_top
            terms[c, ROWS - 2] = -near_bot
            terms[c, ROWS - 1] = 8.0 * near_bot - far_bot
        return terms

    def diff_t(ref, c, r0, n):
        return 8.0 * (ref[c, pl.ds(r0 + 3, n)] - ref[c, pl.ds(r0 + 1, n)]) - (
            ref[c, pl.ds(r0 + 4, n)] - ref[c, pl.ds(r0, n)]
        )

    def diff_p(x):
        return 8.0 * (lane_roll(x, -1) - lane_roll(x, 1)) - (lane_roll(x, -2) - lane_roll(x, 2))

    def diff_r(x):
        return c_up * pltpu.roll(x, LEV - 1, 1) - c_dn * pltpu.roll(x, 1, 1)

    def local_velocity(step, f):
        ref = stress.at[step, f]

        def body(i, carry):
            r0 = i * CHUNK
            own = pl.ds(r0, CHUNK)
            ap, cv = coef[0, own], coef[1, own]
            tt, tr, tp, pp, pr, rr = (ref[c, pl.ds(r0 + 2, CHUNK)] for c in range(6))
            f_t = at * diff_t(ref, TT, r0, CHUNK) + ap * diff_p(tp) + diff_r(tr) + cv * (tt - pp) + (3.0 * ir) * tr
            f_p = at * diff_t(ref, TP, r0, CHUNK) + ap * diff_p(pp) + diff_r(pr) + 2.0 * cv * tp + (3.0 * ir) * pr
            f_r = (
                at * diff_t(ref, TR, r0, CHUNK)
                + ap * diff_p(pr)
                + diff_r(rr)
                + ir * (2.0 * rr - tt - pp)
                + cv * tr
            )
            scale = coef[2, own]
            for c, force in enumerate((f_t, f_p, f_r)):
                value = scale * force
                if step > 0:
                    value = value + vel[step - 1, f, c, pl.ds(r0 + 2, CHUNK)]
                if f == 0:
                    if c == 2:
                        value = value + source[step, own]
                else:
                    value = value + inject[step, c, own]
                part_v[f, c, own] = value
            return carry

        lax.fori_loop(0, ROWS // CHUNK, body, 0)

        if step == 0:
            for c in range(3):
                for row in range(ROWS):
                    part_v[f, c, row] += state_in[f, pl.ds(c * (LEV * ROWS) + row, LEV, stride=ROWS), :]

    BOUNDARY = (0, 1, ROWS - 2, ROWS - 1)
    INNER = tuple(range(2, ROWS - 2))

    def finish_velocity(step, f):
        phase = 2 * step
        rims = rim_terms(phase, f)
        bands = band_terms(phase, f, (1, -1, 1))
        band_of = (TT, TP, TR)
        rim_index = (0, 1, 2)
        copies = []
        for rows in (BOUNDARY, INNER):
            for row in rows:
                for c in range(3):
                    extra = coef[0, row] * rim_of(rims, rim_index[c], row)
                    if rows is BOUNDARY:
                        extra = extra + at * bands[band_of[c], row]
                    vel[step, f, c, 2 + row] = part_v[f, c, row] + coef[2, row] * extra
            if rows is BOUNDARY:
                copies += send_cols(phase + 1, f, vel.at[step, f])
        copies += send_lons(phase + 1, f, lambda c, row: vel[step, f, c, 2 + row])
        return copies

    def local_stress(step, f):
        ref = vel.at[step, f]
        old = stress.at[step, f]

        def body(i, carry):
            r0 = i * CHUNK
            own = pl.ds(r0, CHUNK)
            mid = pl.ds(r0 + 2, CHUNK)
            ap, cv = coef[0, own], coef[1, own]
            lam, mu2 = coef[3, own], coef[4, own]
            vt, vp, vr = (ref[c, mid] for c in range(3))
            e_tt = at * diff_t(ref, 0, r0, CHUNK) + ir * vr
            e_pp = ap * diff_p(vp) + cv * vt + ir * vr
            e_rr = diff_r(vr)
            e_tp = at * diff_t(ref, 1, r0, CHUNK) - cv * vp + ap * diff_p(vt)
            e_tr = diff_r(vt) - ir * vt + at * diff_t(ref, 2, r0, CHUNK)
            e_pr = diff_r(vp) - ir * vp + ap * diff_p(vr)
            dil = lam * (e_tt + e_pp + e_rr)
            half = 0.5 * mu2
            part_s[f, TT, own] = old[TT, mid] + (dil + mu2 * e_tt)
            part_s[f, PP, own] = old[PP, mid] + (dil + mu2 * e_pp)
            part_s[f, RR, own] = old[RR, mid] + (dil + mu2 * e_rr)
            part_s[f, TP, own] = old[TP, mid] + half * e_tp
            part_s[f, TR, own] = old[TR, mid] + half * e_tr
            part_s[f, PR, own] = old[PR, mid] + half * e_pr
            return carry

        lax.fori_loop(0, ROWS // CHUNK, body, 0)

    def finish_stress(step, f):
        phase = 2 * step + 1
        last = step == STEPS - 1
        rims = rim_terms(phase, f)
        bands = band_terms(phase, f, (-1, -1, 1))
        copies = []

        def put(c, row, value):
            if last:
                state_o[f, pl.ds(STATE_OF[c] * (LEV * ROWS) + row, LEV, stride=ROWS), :] = value
            else:
                stress[step + 1, f, c, 2 + row] = value

        for rows in (BOUNDARY, INNER):
            for row in rows:
                ap, lam, mu2 = coef[0, row], coef[3, row], coef[4, row]
                half = 0.5 * mu2
                d_p = [ap * rim_of(rims, c, row) for c in range(3)]
                if rows is BOUNDARY:
                    d_t = [at * bands[c, row] for c in range(3)]
                    dil = lam * (d_t[0] + d_p[1])
                    put(TT, row, part_s[f, TT, row] + (dil + mu2 * d_t[0]))
                    put(TP, row, part_s[f, TP, row] + half * (d_t[1] + d_p[0]))
                    put(TR, row, part_s[f, TR, row] + half * d_t[2])
                else:
                    dil = lam * d_p[1]
                    put(TT, row, part_s[f, TT, row] + dil)
                    put(TP, row, part_s[f, TP, row] + half * d_p[0])
                    put(TR, row, part_s[f, TR, row])
                put(PP, row, part_s[f, PP, row] + (dil + mu2 * d_p[1]))
                put(RR, row, part_s[f, RR, row] + dil)
                put(PR, row, part_s[f, PR, row] + half * d_p[2])
            if rows is BOUNDARY and not last:
                copies += send_cols(phase + 1, f, stress.at[step + 1, f])
        if not last:
            copies += send_lons(phase + 1, f, lambda c, row: stress[step + 1, f, TP + c, 2 + row])
        return copies

    def materials():
        def body(row, carry):
            ids = ids_in[pl.ds(row, LEV, stride=ROWS), :]
            rho = jnp.zeros((LEV, LANES), F32)
            lam, mu = rho, rho
            for layer in range(16):
                hit = ids == layer
                rho = jnp.where(hit, density_ref[layer], rho)
                lam = jnp.where(hit, lame_ref[layer], lam)
                mu = jnp.where(hit, shear_ref[layer], mu)
            coef[2, row] = step_size * (1.0 / rho)
            coef[3, row] = step_size * lam
            coef[4, row] = (2.0 * step_size) * mu
            return carry

        lax.fori_loop(0, ROWS, body, 0)

    def injection():
        plane = lat_cells * lon_cells
        rows = lax.broadcasted_iota(jnp.int32, (ROWS, LEV, LANES), 0) + lat * ROWS
        levels = lax.broadcasted_iota(jnp.int32, (ROWS, LEV, LANES), 1)
        lanes = lax.broadcasted_iota(jnp.int32, (ROWS, LEV, LANES), 2) + lon * LANES
        cell = levels * plane + rows * lon_cells + lanes
        adds = [jnp.zeros((ROWS, LEV, LANES), F32) for _ in range(STEPS)]
        for s in range(src_ref.shape[0]):
            hit = cell == src_ref[s]
            for step in range(STEPS):
                adds[step] = adds[step] + jnp.where(hit, wave_ref[step, s], 0.0)
        for step in range(STEPS):
            source[step] = adds[step]
        cells = cells_ref[...].reshape(1, -1)
        count = cells.shape[1]
        lev_n = lax.div(cells, plane)
        in_plane = cells - lev_n * plane
        row_n = lax.div(in_plane, lon_cells)
        col_n = in_plane - row_n * lon_cells - lon * LANES
        row_n = row_n - lat * ROWS
        inside = (row_n >= 0) & (row_n < ROWS)
        place_n = jnp.where(inside, row_n * LEV + lev_n, -1)
        index = lax.broadcasted_iota(jnp.int32, (LANES, count), 0)
        lane_hot = jnp.where(index == col_n, 1.0, 0.0).astype(jnp.bfloat16)
        place_hit = index == place_n
        for step in range(STEPS):
            for c in range(3):
                values = resid_ref[c, pl.ds(step, 1)]
                high = values.astype(jnp.bfloat16).astype(F32)
                rest = values - high
                middle = rest.astype(jnp.bfloat16).astype(F32)
                total = None
                for term in (high, middle, rest - middle):
                    left_hot = jnp.where(place_hit, term, 0.0).astype(jnp.bfloat16)
                    piece = lax.dot_general(
                        left_hot, lane_hot, (((1,), (1,)), ((), ())), preferred_element_type=F32
                    )
                    total = piece if total is None else total + piece
                inject[step, c] = total.reshape(ROWS, LEV, LANES)

    started = []
    loads[0].wait()
    unpack_state(0)
    loads[1].wait()
    unpack_state(1)
    pl.semaphore_wait(barrier, 4)
    for f in range(2):
        started += send_cols(0, f, stress.at[0, f])
        started += send_lons(0, f, lambda c, row: stress[0, f, TP + c, 2 + row])
    loads[2].wait()
    materials()
    injection()
    outs = []
    for step in range(STEPS):
        for f in range(2):
            local_velocity(step, f)
        for f in range(2):
            wait_halo(2 * step, f)
            started += finish_velocity(step, f)
            local_stress(step, f)
        if step == STEPS - 1:
            for row in range(ROWS):
                density = None
                for s in range(STEPS):
                    for c in range(3):
                        term = vel[s, 0, c, 2 + row] * vel[s, 1, c, 2 + row]
                        density = term if density is None else density + term
                kern_o[pl.ds(row, LEV, stride=ROWS), :] = density
                for f in range(2):
                    for c in range(3):
                        state_o[f, pl.ds(c * (LEV * ROWS) + row, LEV, stride=ROWS), :] = vel[step, f, c, 2 + row]
            velocity_rows = pl.ds(0, 3 * LEV * ROWS)
            stress_rows = pl.ds(3 * LEV * ROWS, 6 * LEV * ROWS)
            outs.append(pltpu.make_async_copy(kern_o, kern_out, out_sem.at[0]))
            for f, out in enumerate((fwd_out, adj_out)):
                outs.append(
                    pltpu.make_async_copy(state_o.at[f, velocity_rows], out.at[velocity_rows], out_sem.at[1 + f])
                )
            for copy in outs:
                copy.start()
        for f in range(2):
            wait_halo(2 * step + 1, f)
            started += finish_stress(step, f)
            if step == STEPS - 1:
                out = (fwd_out, adj_out)[f]
                copy = pltpu.make_async_copy(state_o.at[f, stress_rows], out.at[stress_rows], out_sem.at[3 + f])
                copy.start()
                outs.append(copy)
    for copy in started:
        copy.wait_send()
    for copy in outs:
        copy.wait()


def on_device(n_lon, n_lat, forward, adjoint, layer_ids, density, lame, shear, src, wave, cells, resid):
    flat = 9 * LEV * ROWS
    vmem = pl.BlockSpec(memory_space=pltpu.VMEM)
    smem = pl.BlockSpec(memory_space=pltpu.SMEM)
    hbm = pl.BlockSpec(memory_space=pl.ANY)
    phases = 2 * STEPS
    fwd, adj, kern = pl.pallas_call(
        functools.partial(kernel, n_lon, n_lat),
        out_shape=(
            jax.ShapeDtypeStruct((flat, LANES), F32),
            jax.ShapeDtypeStruct((flat, LANES), F32),
            jax.ShapeDtypeStruct((LEV * ROWS, LANES), F32),
        ),
        in_specs=[hbm, hbm, hbm, smem, smem, smem, smem, smem, vmem, vmem],
        out_specs=(hbm, hbm, hbm),
        scratch_shapes=[
            pltpu.VMEM((2, flat, LANES), F32),
            pltpu.VMEM((LEV * ROWS, LANES), jnp.int32),
            pltpu.VMEM((2, flat, LANES), F32),
            pltpu.VMEM((LEV * ROWS, LANES), F32),
            pltpu.VMEM((STEPS, 2, 6, ROWS + 4, LEV, LANES), F32),
            pltpu.VMEM((STEPS, 2, 3, ROWS + 4, LEV, LANES), F32),
            pltpu.VMEM((2, 3, ROWS, LEV, LANES), F32),
            pltpu.VMEM((2, 6, ROWS, LEV, LANES), F32),
            pltpu.VMEM((STEPS, 3, ROWS, LEV, LANES), F32),
            pltpu.VMEM((STEPS, ROWS, LEV, LANES), F32),
            pltpu.VMEM((5, ROWS, LEV, LANES), F32),
            pltpu.VMEM((phases, 2, 2, 3, 2, LEV, LANES), F32),
            pltpu.VMEM((phases, 2, 2, LEV, LANES), F32),
            pltpu.VMEM((phases, 2, 2, 2, LEV, LANES), F32),
            pltpu.SemaphoreType.DMA((3,)),
            pltpu.SemaphoreType.DMA((5,)),
            pltpu.SemaphoreType.DMA((phases, 2, 2)),
            pltpu.SemaphoreType.DMA((phases, 2, 2)),
            pltpu.SemaphoreType.DMA((phases, 2, 2)),
            pltpu.SemaphoreType.DMA((phases, 2, 2)),
        ],
        compiler_params=pltpu.CompilerParams(collective_id=0, has_side_effects=True),
        name="elastic_steps",
    )(
        forward.reshape(flat, LANES),
        adjoint.reshape(flat, LANES),
        layer_ids.reshape(LEV * ROWS, LANES),
        density,
        lame,
        shear,
        src,
        wave,
        cells,
        jnp.transpose(resid, (1, 0, 2)),
    )
    return fwd.reshape(forward.shape), adj.reshape(adjoint.shape), kern.reshape(layer_ids.shape)


def solution(mesh):
    field = P(None, None, "colat", "lon")
    plane = P(None, "colat", "lon")
    return jax.shard_map(
        functools.partial(on_device, mesh.shape["lon"], mesh.shape["colat"]),
        mesh=mesh,
        in_specs=(field, field, plane) + (P(),) * 7,
        out_specs=(field, field, plane),
        check_vma=False,
    )
```

time: 223 us -> 45.6 us (0.20)
  starting transfers between devices: 79.3 us -> 0 us
  other arithmetic: 59 us -> 0 us
  waiting for transfers between devices: 46 us -> 0 us
  Pallas kernels: 0 us -> 41.2 us
  local copies, waits for them, and re-layouts: 31.1 us -> 3.47 us
  matrix products: 3.89 us -> 0 us
    ppermute x20 -> x0, starting transfers between devices: 79.3 us -> none  [the longest x8 45.4 us: extended(): after = lax.ppermute(leading, axis, down)]
    ppermute x20 -> x0, waiting for transfers between devices: 46 us -> none  [the longest x8 36.9 us: extended(): before = lax.ppermute(last, axis, up)]
    pallas_call x0 -> x1, Pallas kernels: none -> 41.2 us  [on_device(): pl.pallas_call(functools.partial(kernel, n_lon, n_lat), out_shape=(jax.Sh...]
    mul x11 -> x0, other arithmetic: 26.5 us -> none  [the longest x1 10.9 us: on_device(): velocity = velocity + step_size * inv_rho * forcing]
    add x10 -> x0, other arithmetic: 12.4 us -> none  [the longest x1 10.7 us: lookup(): looked + jnp.where(layer_ids == layer_index, values_table[layer_index], 0.0)]
    rev x8 -> x0, local copies, waits for them, and re-layouts: 8.9 us -> none  [the longest x4 4.46 us: fold_pole(): padded[..., rim_width:2 * rim_width, :][..., ::-1, :] * sign_flip]
    slice x11 -> x0, local copies, waits for them, and re-layouts: 8.57 us -> none  [the longest x5 4.54 us: extended(): leading = lax.slice_in_dim(array, 0, width, axis=dim)]
    div x10 -> x0, other arithmetic: 8.57 us -> none  [the longest x4 4.53 us: diff_phi(): (8.0 * (values[..., 2:-2, 3:-1] - values[..., 2:-2, 1:-3]) - (values[...,...]
  transfers between devices with their start and end apart: 20 -> 0, of which waited for: 12 -> 0; matrix products, arithmetic and copies ran while one was open for 24% -> 0% of each run, Pallas kernels for 0% -> 0%
where the time goes in v1:
time: 45.6 us; the launch traced here: 45.3 us
  Pallas kernels  41.2 us (90%)
  local copies, waits for them, and re-layouts  3.47 us (8%)
  between operations  0.65 us (1%)
    pallas_call x1, Pallas kernels, on_device(): pl.pallas_call(functools.partial(kernel, n_lon, n_lat), out_shape=(jax.Sh...  41.2 us
    unnamed x7, local copies, waits for them, and re-layouts  3.47 us

profile of v1, /device:TPU:8, one launch (start us, length us, event | category | flops | bytes accessed | tf_op | source)
XLA Modules:
  0.0 45.3 jit_solution(483427803832443156)
XLA Ops:
  0.6 41.2 %elastic_steps.1 = (f32[1152,128]{1,0:T(8,128)}, f32[1152,128]{1,0:T(8,128)}, f32[128,128]{1,0:T(8,128)}) custom-call(f32[1152,128]{1,0:T(8,128)} %bitcast.7, f32[1152,128]{1,0:T(8,128)} %bitcast.8, s32[128,128]{1,0:T(8,128)} %bitcast.11, f32[16]{0:T(128)} %density_ref.1, f32[16]{0:T(128)} %lame_ref.1, f32[16]{0:T(128)} %shear_ref.1, s32[8]{0:T(128)} %src_ref.1, ...), custom_call_target="tpu_custom_call" | custom-call | tf_op jit(solution)/shard_map/elastic_steps/pallas_call | solution.py:492
  41.8 0.0 copy-start
  41.8 2.0 %copy.16 = f32[9,8,16,128]{3,2,1,0:T(8,128)} copy(f32[9,8,16,128]{3,2,1,0:T(8,128)} %bitcast.10) | data formatting | bytes 1179648
  43.8 0.0 copy-done
  43.8 0.0 copy-start.1
  43.8 0.8 %copy.17 = f32[9,8,16,128]{3,2,1,0:T(8,128)} copy(f32[9,8,16,128]{3,2,1,0:T(8,128)S(1)} %bitcast.9) | data formatting | bytes 1179648
  44.6 0.0 copy-done.1
  44.7 0.6 %copy.18 = f32[8,16,128]{2,1,0:T(8,128)} copy(f32[8,16,128]{2,1,0:T(8,128)S(1)} %bitcast.12) | data formatting | bytes 131072
Async XLA Ops:
  41.8 2.0 %copy-start = (f32[1152,128]{1,0:T(8,128)S(1)}, f32[1152,128]{1,0:T(8,128)}, u32[]{:S(2)}) copy-start(f32[1152,128]{1,0:T(8,128)} %get-tuple-element.7) | copy-start | bytes 1769476
  43.8 0.9 %copy-start.1 = (f32[128,128]{1,0:T(8,128)S(1)}, f32[128,128]{1,0:T(8,128)}, u32[]{:S(2)}) copy-start(f32[128,128]{1,0:T(8,128)} %get-tuple-element.8) | copy-start | bytes 196612

commit v2 on v1

--- a/solution.py
+++ b/solution.py
@@ -38,13 +38,10 @@
     wave_ref,
     cells_ref,
     resid_ref,
-    fwd_out,
-    adj_out,
-    kern_out,
+    state_o,
+    kern_o,
     state_in,
     ids_in,
-    state_o,
-    kern_o,
     stress,
     vel,
     part_v,
@@ -52,11 +49,12 @@
     inject,
     source,
     coef,
+    part_rim,
+    coef_rim,
     col_recv,
     lon_send,
     lon_recv,
     in_sem,
-    out_sem,
     col_ssem,
     col_rsem,
     lon_ssem,
@@ -84,10 +82,14 @@
     for peer in (up, down, to_left, to_right):
         pl.semaphore_signal(barrier, inc=1, device_id=peer, device_id_type=MESH)
 
+    velocity_rows = pl.ds(0, 3 * LEV * ROWS)
+    stress_rows = pl.ds(3 * LEV * ROWS, 6 * LEV * ROWS)
     loads = [
-        pltpu.make_async_copy(fwd_hbm, state_in.at[0], in_sem.at[0]),
-        pltpu.make_async_copy(adj_hbm, state_in.at[1], in_sem.at[1]),
+        pltpu.make_async_copy(fwd_hbm.at[stress_rows], state_in.at[0, stress_rows], in_sem.at[0]),
+        pltpu.make_async_copy(adj_hbm.at[stress_rows], state_in.at[1, stress_rows], in_sem.at[1]),
         pltpu.make_async_copy(ids_hbm, ids_in, in_sem.at[2]),
+        pltpu.make_async_copy(fwd_hbm.at[velocity_rows], state_in.at[0, velocity_rows], in_sem.at[3]),
+        pltpu.make_async_copy(adj_hbm.at[velocity_rows], state_in.at[1, velocity_rows], in_sem.at[4]),
     ]
     for load in loads:
         load.start()
@@ -117,9 +119,12 @@
             vel[step, f, :, 0:2] = zero
             vel[step, f, :, ROWS + 2 : ROWS + 4] = zero
 
-    def unpack_state(f):
-        for c in range(6):
-            for row in range(ROWS):
+    BOUNDARY = (0, 1, ROWS - 2, ROWS - 1)
+    INNER = tuple(range(2, ROWS - 2))
+
+    def unpack_stress(f, comps, rows):
+        for c in comps:
+            for row in rows:
                 start = STATE_OF[c] * (LEV * ROWS) + row
                 stress[0, f, c, 2 + row] = state_in[f, pl.ds(start, LEV, stride=ROWS), :]
 
@@ -148,21 +153,20 @@
     quad = lax.div(lane, 4)
     spot = lax.rem(lane, 4)
 
-    def pack_rim(rows_of):
+    def pack_rim(base, rows, row_of):
         packed = []
         for group in range(2):
-            acc = jnp.zeros((LEV, LANES), F32)
+            acc = base[group]
             for slot in range(32):
-                k = group * 32 + slot
-                if k < 48:
-                    acc = jnp.where(quad == slot, lane_roll(rows_of(k // ROWS, k % ROWS), 4 * slot + 2), acc)
+                c, row = divmod(group * 32 + slot, ROWS)
+                if c < 3 and row in rows:
+                    acc = jnp.where(quad == slot, lane_roll(row_of(c, row), 4 * slot + 2), acc)
             packed.append(acc)
         return packed
 
-    def send_lons(phase, f, rows_of):
-        packed = pack_rim(rows_of)
-        for group in range(2):
-            lon_send[phase, f, group] = packed[group]
+    blank = [jnp.zeros((LEV, LANES), F32)] * 2
+
+    def send_lons(phase, f):
         copies = []
         for slot, peer in ((0, to_right), (1, to_left)):
             copy = pltpu.make_async_remote_copy(
@@ -282,28 +286,36 @@
             for c in range(3):
                 for row in range(ROWS):
                     part_v[f, c, row] += state_in[f, pl.ds(c * (LEV * ROWS) + row, LEV, stride=ROWS), :]
-
-    BOUNDARY = (0, 1, ROWS - 2, ROWS - 1)
-    INNER = tuple(range(2, ROWS - 2))
-
-    def finish_velocity(step, f):
+        packed = pack_rim(blank, INNER, lambda c, row: part_v[f, c, row])
+        for group in range(2):
+            part_rim[f, group] = packed[group]
+
+    def send_finished(phase, f, kind, rims, ref, lon_row):
+        base = [part_rim[f, group] + coef_rim[kind, group] * rims[group] for group in range(2)]
+        packed = pack_rim(base, BOUNDARY, lon_row)
+        for group in range(2):
+            lon_send[phase + 1, f, group] = packed[group]
+        return send_cols(phase + 1, f, ref) + send_lons(phase + 1, f)
+
+    def finish_velocity(step, f, rows, rims, bands=None):
+        band_of = (TT, TP, TR)
+        done = {}
+        for row in rows:
+            for c in range(3):
+                extra = coef[0, row] * rim_of(rims, c, row)
+                if bands is not None:
+                    extra = extra + at * bands[band_of[c], row]
+                done[c, row] = part_v[f, c, row] + coef[2, row] * extra
+                vel[step, f, c, 2 + row] = done[c, row]
+        return done
+
+    def edges_velocity(step, f):
         phase = 2 * step
+        wait_halo(phase, f)
         rims = rim_terms(phase, f)
-        bands = band_terms(phase, f, (1, -1, 1))
-        band_of = (TT, TP, TR)
-        rim_index = (0, 1, 2)
-        copies = []
-        for rows in (BOUNDARY, INNER):
-            for row in rows:
-                for c in range(3):
-                    extra = coef[0, row] * rim_of(rims, rim_index[c], row)
-                    if rows is BOUNDARY:
-                        extra = extra + at * bands[band_of[c], row]
-                    vel[step, f, c, 2 + row] = part_v[f, c, row] + coef[2, row] * extra
-            if rows is BOUNDARY:
-                copies += send_cols(phase + 1, f, vel.at[step, f])
-        copies += send_lons(phase + 1, f, lambda c, row: vel[step, f, c, 2 + row])
-        return copies
+        done = finish_velocity(step, f, BOUNDARY, rims, band_terms(phase, f, (1, -1, 1)))
+        copies = send_finished(phase, f, 0, rims, vel.at[step, f], lambda c, row: done[c, row])
+        return rims, copies
 
     def local_stress(step, f):
         ref = vel.at[step, f]
@@ -333,44 +345,56 @@
             return carry
 
         lax.fori_loop(0, ROWS // CHUNK, body, 0)
-
-    def finish_stress(step, f):
-        phase = 2 * step + 1
+        if step < STEPS - 1:
+            packed = pack_rim(blank, INNER, lambda c, row: part_s[f, TP + c, row])
+            for group in range(2):
+                part_rim[f, group] = packed[group]
+        else:
+            for row in INNER:
+                start = STATE_OF[TR] * (LEV * ROWS) + row
+                state_o[f, pl.ds(start, LEV, stride=ROWS), :] = part_s[f, TR, row]
+
+    def finish_stress(step, f, rows, rims, bands=None):
         last = step == STEPS - 1
-        rims = rim_terms(phase, f)
-        bands = band_terms(phase, f, (-1, -1, 1))
-        copies = []
+        done = {}
 
         def put(c, row, value):
+            done[c, row] = value
             if last:
                 state_o[f, pl.ds(STATE_OF[c] * (LEV * ROWS) + row, LEV, stride=ROWS), :] = value
             else:
                 stress[step + 1, f, c, 2 + row] = value
 
-        for rows in (BOUNDARY, INNER):
-            for row in rows:
-                ap, lam, mu2 = coef[0, row], coef[3, row], coef[4, row]
-                half = 0.5 * mu2
-                d_p = [ap * rim_of(rims, c, row) for c in range(3)]
-                if rows is BOUNDARY:
-                    d_t = [at * bands[c, row] for c in range(3)]
-                    dil = lam * (d_t[0] + d_p[1])
-                    put(TT, row, part_s[f, TT, row] + (dil + mu2 * d_t[0]))
-                    put(TP, row, part_s[f, TP, row] + half * (d_t[1] + d_p[0]))
-                    put(TR, row, part_s[f, TR, row] + half * d_t[2])
-                else:
-                    dil = lam * d_p[1]
-                    put(TT, row, part_s[f, TT, row] + dil)
-                    put(TP, row, part_s[f, TP, row] + half * d_p[0])
+        for row in rows:
+            ap, lam, mu2 = coef[0, row], coef[3, row], coef[4, row]
+            half = 0.5 * mu2
+            d_p = [ap * rim_of(rims, c, row) for c in range(3)]
+            if bands is not None:
+                d_t = [at * bands[c, row] for c in range(3)]
+                dil = lam * (d_t[0] + d_p[1])
+                put(TT, row, part_s[f, TT, row] + (dil + mu2 * d_t[0]))
+                put(TP, row, part_s[f, TP, row] + half * (d_t[1] + d_p[0]))
+                put(TR, row, part_s[f, TR, row] + half * d_t[2])
+            else:
+                dil = lam * d_p[1]
+                put(TT, row, part_s[f, TT, row] + dil)
+                put(TP, row, part_s[f, TP, row] + half * d_p[0])
+                if not last:
                     put(TR, row, part_s[f, TR, row])
-                put(PP, row, part_s[f, PP, row] + (dil + mu2 * d_p[1]))
-                put(RR, row, part_s[f, RR, row] + dil)
-                put(PR, row, part_s[f, PR, row] + half * d_p[2])
-            if rows is BOUNDARY and not last:
-                copies += send_cols(phase + 1, f, stress.at[step + 1, f])
-        if not last:
-            copies += send_lons(phase + 1, f, lambda c, row: stress[step + 1, f, TP + c, 2 + row])
-        return copies
+            put(PP, row, part_s[f, PP, row] + (dil + mu2 * d_p[1]))
+            put(RR, row, part_s[f, RR, row] + dil)
+            put(PR, row, part_s[f, PR, row] + half * d_p[2])
+        return done
+
+    def edges_stress(step, f):
+        phase = 2 * step + 1
+        wait_halo(phase, f)
+        rims = rim_terms(phase, f)
+        done = finish_stress(step, f, BOUNDARY, rims, band_terms(phase, f, (-1, -1, 1)))
+        copies = []
+        if step < STEPS - 1:
+            copies = send_finished(phase, f, 1, rims, stress.at[step + 1, f], lambda c, row: done[TP + c, row])
+        return rims, copies
 
     def materials():
         def body(row, carry):
@@ -388,6 +412,17 @@
             return carry
 
         lax.fori_loop(0, ROWS, body, 0)
+        packed = (
+            pack_rim(blank, INNER, lambda c, row: coef[2, row] * coef[0, row]),
+            pack_rim(
+                blank,
+                INNER,
+                lambda c, row: coef[0, row] * (coef[3, row] + coef[4, row] if c == 1 else 0.5 * coef[4, row]),
+            ),
+        )
+        for kind in range(2):
+            for group in range(2):
+                coef_rim[kind, group] = packed[kind][group]
 
     def injection():
         plane = lat_cells * lon_cells
@@ -430,24 +465,33 @@
                 inject[step, c] = total.reshape(ROWS, LEV, LANES)
 
     started = []
-    loads[0].wait()
-    unpack_state(0)
-    loads[1].wait()
-    unpack_state(1)
+    for f in range(2):
+        loads[f].wait()
+        unpack_stress(f, range(3), BOUNDARY)
     pl.semaphore_wait(barrier, 4)
     for f in range(2):
         started += send_cols(0, f, stress.at[0, f])
-        started += send_lons(0, f, lambda c, row: stress[0, f, TP + c, 2 + row])
-    loads[2].wait()
+    for f in range(2):
+        unpack_stress(f, range(3), INNER)
+        unpack_stress(f, range(3, 6), range(ROWS))
+        packed = pack_rim(blank, range(ROWS), lambda c, row: stress[0, f, TP + c, 2 + row])
+        for group in range(2):
+            lon_send[0, f, group] = packed[group]
+        started += send_lons(0, f)
+    for load in loads[2:]:
+        load.wait()
     materials()
     injection()
-    outs = []
     for step in range(STEPS):
         for f in range(2):
             local_velocity(step, f)
+        rims = []
         for f in range(2):
-            wait_halo(2 * step, f)
-            started += finish_velocity(step, f)
+            rim, copies = edges_velocity(step, f)
+            rims.append(rim)
+            started += copies
+        for f in range(2):
+            finish_velocity(step, f, INNER, rims[f])
             local_stress(step, f)
         if step == STEPS - 1:
             for row in range(ROWS):
@@ -460,26 +504,26 @@
                 for f in range(2):
                     for c in range(3):
                         state_o[f, pl.ds(c * (LEV * ROWS) + row, LEV, stride=ROWS), :] = vel[step, f, c, 2 + row]
-            velocity_rows = pl.ds(0, 3 * LEV * ROWS)
-            stress_rows = pl.ds(3 * LEV * ROWS, 6 * LEV * ROWS)
-            outs.append(pltpu.make_async_copy(kern_o, kern_out, out_sem.at[0]))
-            for f, out in enumerate((fwd_out, adj_out)):
-                outs.append(
-                    pltpu.make_async_copy(state_o.at[f, velocity_rows], out.at[velocity_rows], out_sem.at[1 + f])
-                )
-            for copy in outs:
-                copy.start()
+        rims = []
         for f in range(2):
-            wait_halo(2 * step + 1, f)
-            started += finish_stress(step, f)
-            if step == STEPS - 1:
-                out = (fwd_out, adj_out)[f]
-                copy = pltpu.make_async_copy(state_o.at[f, stress_rows], out.at[stress_rows], out_sem.at[3 + f])
-                copy.start()
-                outs.append(copy)
+            rim, copies = edges_stress(step, f)
+            rims.append(rim)
+            started += copies
+        for f in range(2):
+            finish_stress(step, f, INNER, rims[f])
     for copy in started:
         copy.wait_send()
-    for copy in outs:
+
+
+def store(state_ref, kern_ref, fwd_out, adj_out, kern_out, sem):
+    copies = [
+        pltpu.make_async_copy(state_ref.at[0], fwd_out, sem.at[0]),
+        pltpu.make_async_copy(state_ref.at[1], adj_out, sem.at[1]),
+        pltpu.make_async_copy(kern_ref, kern_out, sem.at[2]),
+    ]
+    for copy in copies:
+        copy.start()
+    for copy in copies:
         copy.wait()
 
 
@@ -489,20 +533,14 @@
     smem = pl.BlockSpec(memory_space=pltpu.SMEM)
     hbm = pl.BlockSpec(memory_space=pl.ANY)
     phases = 2 * STEPS
-    fwd, adj, kern = pl.pallas_call(
+    state, kern = pl.pallas_call(
         functools.partial(kernel, n_lon, n_lat),
-        out_shape=(
-            jax.ShapeDtypeStruct((flat, LANES), F32),
-            jax.ShapeDtypeStruct((flat, LANES), F32),
-            jax.ShapeDtypeStruct((LEV * ROWS, LANES), F32),
-        ),
+        out_shape=(pltpu.VMEM((2, flat, LANES), F32), pltpu.VMEM((LEV * ROWS, LANES), F32)),
         in_specs=[hbm, hbm, hbm, smem, smem, smem, smem, smem, vmem, vmem],
-        out_specs=(hbm, hbm, hbm),
+        out_specs=(vmem, vmem),
         scratch_shapes=[
             pltpu.VMEM((2, flat, LANES), F32),
             pltpu.VMEM((LEV * ROWS, LANES), jnp.int32),
-            pltpu.VMEM((2, flat, LANES), F32),
-            pltpu.VMEM((LEV * ROWS, LANES), F32),
             pltpu.VMEM((STEPS, 2, 6, ROWS + 4, LEV, LANES), F32),
             pltpu.VMEM((STEPS, 2, 3, ROWS + 4, LEV, LANES), F32),
             pltpu.VMEM((2, 3, ROWS, LEV, LANES), F32),
@@ -510,10 +548,11 @@
             pltpu.VMEM((STEPS, 3, ROWS, LEV, LANES), F32),
             pltpu.VMEM((STEPS, ROWS, LEV, LANES), F32),
             pltpu.VMEM((5, ROWS, LEV, LANES), F32),
+            pltpu.VMEM((2, 2, LEV, LANES), F32),
+            pltpu.VMEM((2, 2, LEV, LANES), F32),
             pltpu.VMEM((phases, 2, 2, 3, 2, LEV, LANES), F32),
             pltpu.VMEM((phases, 2, 2, LEV, LANES), F32),
             pltpu.VMEM((phases, 2, 2, 2, LEV, LANES), F32),
-            pltpu.SemaphoreType.DMA((3,)),
             pltpu.SemaphoreType.DMA((5,)),
             pltpu.SemaphoreType.DMA((phases, 2, 2)),
             pltpu.SemaphoreType.DMA((phases, 2, 2)),
@@ -534,6 +573,19 @@
         cells,
         jnp.transpose(resid, (1, 0, 2)),
     )
+    fwd, adj, kern = pl.pallas_call(
+        store,
+        out_shape=(
+            jax.ShapeDtypeStruct((flat, LANES), F32),
+            jax.ShapeDtypeStruct((flat, LANES), F32),
+            jax.ShapeDtypeStruct((LEV * ROWS, LANES), F32),
+        ),
+        in_specs=[vmem, vmem],
+        out_specs=(hbm, hbm, hbm),
+        scratch_shapes=[pltpu.SemaphoreType.DMA((3,))],
+        compiler_params=pltpu.CompilerParams(vmem_limit_bytes=1 << 20),
+        name="store",
+    )(pltpu.with_memory_space_constraint(state, pltpu.VMEM), pltpu.with_memory_space_constraint(kern, pltpu.VMEM))
     return fwd.reshape(forward.shape), adj.reshape(adjoint.shape), kern.reshape(layer_ids.shape)
 
 

time: 45.6 us -> 42.4 us (0.930)
  local copies, waits for them, and re-layouts: 3.47 us -> 0 us
    unnamed x7 -> x0, local copies, waits for them, and re-layouts: 3.47 us -> none
    pallas_call x1 -> x2, Pallas kernels: 41.2 us -> 41.5 us  [the longest x1 40.5 us: on_device(): pl.pallas_call(functools.partial(kernel, n_lon, n_lat), out_shape=(pltpu....]
where the time goes in v2:
time: 42.4 us; the launch traced here: 42.1 us
  Pallas kernels  41.5 us (98%)
  between operations  0.64 us (2%)
    pallas_call x1, Pallas kernels, on_device(): pl.pallas_call(functools.partial(kernel, n_lon, n_lat), out_shape=(pltpu....  40.5 us
    pallas_call x1, Pallas kernels, on_device(): pl.pallas_call(store, out_shape=(jax.ShapeDtypeStruct((flat, LANES), F32)...  1.05 us

profile of v2, /device:TPU:8, one launch (start us, length us, event | category | flops | bytes accessed | tf_op | source)
XLA Modules:
  0.0 42.1 jit_solution(1811979148804077182)
XLA Ops:
  0.6 40.5 %elastic_steps.1 = (f32[2,1152,128]{2,1,0:T(8,128)S(1)}, f32[128,128]{1,0:T(8,128)S(1)}) custom-call(f32[1152,128]{1,0:T(8,128)} %bitcast.7, f32[1152,128]{1,0:T(8,128)} %bitcast.8, s32[128,128]{1,0:T(8,128)} %bitcast.9, f32[16]{0:T(128)} %density_ref.1, f32[16]{0:T(128)} %lame_ref.1, f32[16]{0:T(128)} %shear_ref.1, s32[8]{0:T(128)} %src_ref.1, ...), custom_call_target="tpu_custom_call" | custom-call | tf_op jit(solution)/shard_map/elastic_steps/pallas_call | solution.py:536
  41.1 1.0 %store.1 = (f32[1152,128]{1,0:T(8,128)}, f32[1152,128]{1,0:T(8,128)}, f32[128,128]{1,0:T(8,128)}) custom-call(f32[2,1152,128]{2,1,0:T(8,128)S(1)} %get-tuple-element.8.state_ref, f32[128,128]{1,0:T(8,128)S(1)} %get-tuple-element.9.kern_ref), custom_call_target="tpu_custom_call" | custom-call | tf_op jit(solution)/shard_map/store/pallas_call | solution.py:576

commit v3 on v2

--- a/solution.py
+++ b/solution.py
@@ -54,11 +54,22 @@
     col_recv,
     lon_send,
     lon_recv,
+    zone,
+    zcoef,
+    zinject,
+    zdensity,
+    own_pack,
+    own_recv,
+    strip_pack,
+    strip_mid,
+    strip_recv,
     in_sem,
     col_ssem,
     col_rsem,
     lon_ssem,
     lon_rsem,
+    zone_ssem,
+    zone_rsem,
 ):
     lon = lax.axis_index("lon")
     lat = lax.axis_index("colat")
@@ -78,9 +89,32 @@
     to_left = {"lon": left, "colat": lat}
     to_right = {"lon": right, "colat": lat}
 
+    half = n_lon // 2
+    place_in_half = lax.rem(lon, half)
+    is_e = 1 - lax.div(place_in_half + half - 1, half)
+    is_w = lax.div(place_in_half + 1, half)
+    at_seam = is_e + is_w
+    beside = lax.rem(lon + n_lon - is_e + is_w, n_lon)
+    across = {"lon": beside, "colat": lat}
+    across_up = {"lon": lax.rem(beside + is_top * half, n_lon), "colat": lat - 1 + is_top}
+    across_down = {"lon": lax.rem(beside + is_bot * half, n_lon), "colat": lat + 1 - is_bot}
+
     barrier = pltpu.get_barrier_semaphore()
-    for peer in (up, down, to_left, to_right):
+
+    def greet(peer):
         pl.semaphore_signal(barrier, inc=1, device_id=peer, device_id_type=MESH)
+
+    for peer in (up, down, to_left):
+        greet(peer)
+
+    @pl.when(is_w == 0)
+    def _():
+        greet(to_right)
+
+    @pl.when(is_e == 1)
+    def _():
+        greet(across_up)
+        greet(across_down)
 
     velocity_rows = pl.ds(0, 3 * LEV * ROWS)
     stress_rows = pl.ds(3 * LEV * ROWS, 6 * LEV * ROWS)
@@ -121,12 +155,14 @@
 
     BOUNDARY = (0, 1, ROWS - 2, ROWS - 1)
     INNER = tuple(range(2, ROWS - 2))
+    INNER_GROUPS = tuple(INNER[i : i + 4] for i in range(0, len(INNER), 4))
 
     def unpack_stress(f, comps, rows):
         for c in comps:
-            for row in rows:
-                start = STATE_OF[c] * (LEV * ROWS) + row
-                stress[0, f, c, 2 + row] = state_in[f, pl.ds(start, LEV, stride=ROWS), :]
+            first = STATE_OF[c] * (LEV * ROWS)
+            values = [state_in[f, pl.ds(first + row, LEV, stride=ROWS), :] for row in rows]
+            for row, value in zip(rows, values):
+                stress[0, f, c, 2 + row] = value
 
     def send_cols(phase, f, ref):
         dst_slot = 1 - is_top
@@ -166,23 +202,25 @@
 
     blank = [jnp.zeros((LEV, LANES), F32)] * 2
 
+    def lon_copy(phase, f, slot):
+        return pltpu.make_async_remote_copy(
+            src_ref=lon_send.at[phase, f],
+            dst_ref=lon_recv.at[phase, f, slot],
+            send_sem=lon_ssem.at[phase, f, slot],
+            recv_sem=lon_rsem.at[phase, f, slot],
+            device_id=(to_right, to_left)[slot],
+            device_id_type=MESH,
+        )
+
     def send_lons(phase, f):
-        copies = []
-        for slot, peer in ((0, to_right), (1, to_left)):
-            copy = pltpu.make_async_remote_copy(
-                src_ref=lon_send.at[phase, f],
-                dst_ref=lon_recv.at[phase, f, slot],
-                send_sem=lon_ssem.at[phase, f, slot],
-                recv_sem=lon_rsem.at[phase, f, slot],
-                device_id=peer,
-                device_id_type=MESH,
-            )
-            copy.start()
-            copies.append(copy)
-        return copies
+        for slot, seam in ((0, is_w), (1, is_e)):
+
+            @pl.when(seam == 0)
+            def _():
+                lon_copy(phase, f, slot).start()
 
     def wait_halo(phase, f):
-        for slot in range(2):
+        for slot, seam in ((0, is_e), (1, is_w)):
             pltpu.make_async_remote_copy(
                 src_ref=col_recv.at[phase, f, slot],
                 dst_ref=col_recv.at[phase, f, slot],
@@ -191,20 +229,18 @@
                 device_id=up,
                 device_id_type=MESH,
             ).wait_recv()
-            pltpu.make_async_remote_copy(
-                src_ref=lon_send.at[phase, f],
-                dst_ref=lon_recv.at[phase, f, slot],
-                send_sem=lon_ssem.at[phase, f, slot],
-                recv_sem=lon_rsem.at[phase, f, slot],
-                device_id=to_left,
-                device_id_type=MESH,
-            ).wait_recv()
+
+            @pl.when(seam == 0)
+            def _():
+                lon_copy(phase, f, slot).wait_recv()
 
     def rim_terms(phase, f):
         out = []
         for group in range(2):
             own = lon_send[phase, f, group]
-            halo = jnp.where(spot < 2, lon_recv[phase, f, 0, group], lon_recv[phase, f, 1, group]) - own
+            from_left = jnp.where(is_e == 1, own, lon_recv[phase, f, 0, group])
+            from_right = jnp.where(is_w == 1, own, lon_recv[phase, f, 1, group])
+            halo = jnp.where(spot < 2, from_left, from_right) - own
             next1, next2 = lane_roll(halo, -1), lane_roll(halo, -2)
             prev1, prev2 = lane_roll(halo, 1), lane_roll(halo, 2)
             term = jnp.where(
@@ -250,25 +286,48 @@
     def diff_r(x):
         return c_up * pltpu.roll(x, LEV - 1, 1) - c_dn * pltpu.roll(x, 1, 1)
 
+    def force_terms(ref, index, cref, r0):
+        own = pl.ds(r0, CHUNK)
+        ap, cv = cref[0, own], cref[1, own]
+        tt, tr, tp, pp, pr, rr = (ref[index[c], pl.ds(r0 + 2, CHUNK)] for c in range(6))
+        return (
+            at * diff_t(ref, index[TT], r0, CHUNK)
+            + ap * diff_p(tp)
+            + diff_r(tr)
+            + cv * (tt - pp)
+            + (3.0 * ir) * tr,
+            at * diff_t(ref, index[TP], r0, CHUNK) + ap * diff_p(pp) + diff_r(pr) + 2.0 * cv * tp + (3.0 * ir) * pr,
+            at * diff_t(ref, index[TR], r0, CHUNK)
+            + ap * diff_p(pr)
+            + diff_r(rr)
+            + ir * (2.0 * rr - tt - pp)
+            + cv * tr,
+        )
+
+    def stress_terms(ref, cref, r0):
+        own = pl.ds(r0, CHUNK)
+        ap, cv = cref[0, own], cref[1, own]
+        lam, mu2 = cref[3, own], cref[4, own]
+        vt, vp, vr = (ref[c, pl.ds(r0 + 2, CHUNK)] for c in range(3))
+        e_tt = at * diff_t(ref, 0, r0, CHUNK) + ir * vr
+        e_pp = ap * diff_p(vp) + cv * vt + ir * vr
+        e_rr = diff_r(vr)
+        e_tp = at * diff_t(ref, 1, r0, CHUNK) - cv * vp + ap * diff_p(vt)
+        e_tr = diff_r(vt) - ir * vt + at * diff_t(ref, 2, r0, CHUNK)
+        e_pr = diff_r(vp) - ir * vp + ap * diff_p(vr)
+        dil = lam * (e_tt + e_pp + e_rr)
+        shear = 0.5 * mu2
+        return (dil + mu2 * e_tt, shear * e_tr, shear * e_tp, dil + mu2 * e_pp, shear * e_pr, dil + mu2 * e_rr)
+
     def local_velocity(step, f):
         ref = stress.at[step, f]
 
         def body(i, carry):
             r0 = i * CHUNK
             own = pl.ds(r0, CHUNK)
-            ap, cv = coef[0, own], coef[1, own]
-            tt, tr, tp, pp, pr, rr = (ref[c, pl.ds(r0 + 2, CHUNK)] for c in range(6))
-            f_t = at * diff_t(ref, TT, r0, CHUNK) + ap * diff_p(tp) + diff_r(tr) + cv * (tt - pp) + (3.0 * ir) * tr
-            f_p = at * diff_t(ref, TP, r0, CHUNK) + ap * diff_p(pp) + diff_r(pr) + 2.0 * cv * tp + (3.0 * ir) * pr
-            f_r = (
-                at * diff_t(ref, TR, r0, CHUNK)
-                + ap * diff_p(pr)
-                + diff_r(rr)
-                + ir * (2.0 * rr - tt - pp)
-                + cv * tr
-            )
+            forces = force_terms(ref, range(6), coef, r0)
             scale = coef[2, own]
-            for c, force in enumerate((f_t, f_p, f_r)):
+            for c, force in enumerate(forces):
                 value = scale * force
                 if step > 0:
                     value = value + vel[step - 1, f, c, pl.ds(r0 + 2, CHUNK)]
@@ -284,8 +343,12 @@
 
         if step == 0:
             for c in range(3):
+                values = [
+                    part_v[f, c, row] + state_in[f, pl.ds(c * (LEV * ROWS) + row, LEV, stride=ROWS), :]
+                    for row in range(ROWS)
+                ]
                 for row in range(ROWS):
-                    part_v[f, c, row] += state_in[f, pl.ds(c * (LEV * ROWS) + row, LEV, stride=ROWS), :]
+                    part_v[f, c, row] = values[row]
         packed = pack_rim(blank, INNER, lambda c, row: part_v[f, c, row])
         for group in range(2):
             part_rim[f, group] = packed[group]
@@ -295,7 +358,9 @@
         packed = pack_rim(base, BOUNDARY, lon_row)
         for group in range(2):
             lon_send[phase + 1, f, group] = packed[group]
-        return send_cols(phase + 1, f, ref) + send_lons(phase + 1, f)
+        copies = send_cols(phase + 1, f, ref)
+        send_lons(phase + 1, f)
+        return copies
 
     def finish_velocity(step, f, rows, rims, bands=None):
         band_of = (TT, TP, TR)
@@ -306,7 +371,8 @@
                 if bands is not None:
                     extra = extra + at * bands[band_of[c], row]
                 done[c, row] = part_v[f, c, row] + coef[2, row] * extra
-                vel[step, f, c, 2 + row] = done[c, row]
+        for (c, row), value in done.items():
+            vel[step, f, c, 2 + row] = value
         return done
 
     def edges_velocity(step, f):
@@ -324,24 +390,8 @@
         def body(i, carry):
             r0 = i * CHUNK
             own = pl.ds(r0, CHUNK)
-            mid = pl.ds(r0 + 2, CHUNK)
-            ap, cv = coef[0, own], coef[1, own]
-            lam, mu2 = coef[3, own], coef[4, own]
-            vt, vp, vr = (ref[c, mid] for c in range(3))
-            e_tt = at * diff_t(ref, 0, r0, CHUNK) + ir * vr
-            e_pp = ap * diff_p(vp) + cv * vt + ir * vr
-            e_rr = diff_r(vr)
-            e_tp = at * diff_t(ref, 1, r0, CHUNK) - cv * vp + ap * diff_p(vt)
-            e_tr = diff_r(vt) - ir * vt + at * diff_t(ref, 2, r0, CHUNK)
-            e_pr = diff_r(vp) - ir * vp + ap * diff_p(vr)
-            dil = lam * (e_tt + e_pp + e_rr)
-            half = 0.5 * mu2
-            part_s[f, TT, own] = old[TT, mid] + (dil + mu2 * e_tt)
-            part_s[f, PP, own] = old[PP, mid] + (dil + mu2 * e_pp)
-            part_s[f, RR, own] = old[RR, mid] + (dil + mu2 * e_rr)
-            part_s[f, TP, own] = old[TP, mid] + half * e_tp
-            part_s[f, TR, own] = old[TR, mid] + half * e_tr
-            part_s[f, PR, own] = old[PR, mid] + half * e_pr
+            for c, rate in enumerate(stress_terms(ref, coef, r0)):
+                part_s[f, c, own] = old[c, pl.ds(r0 + 2, CHUNK)] + rate
             return carry
 
         lax.fori_loop(0, ROWS // CHUNK, body, 0)
@@ -349,10 +399,6 @@
             packed = pack_rim(blank, INNER, lambda c, row: part_s[f, TP + c, row])
             for group in range(2):
                 part_rim[f, group] = packed[group]
-        else:
-            for row in INNER:
-                start = STATE_OF[TR] * (LEV * ROWS) + row
-                state_o[f, pl.ds(start, LEV, stride=ROWS), :] = part_s[f, TR, row]
 
     def finish_stress(step, f, rows, rims, bands=None):
         last = step == STEPS - 1
@@ -360,10 +406,6 @@
 
         def put(c, row, value):
             done[c, row] = value
-            if last:
-                state_o[f, pl.ds(STATE_OF[c] * (LEV * ROWS) + row, LEV, stride=ROWS), :] = value
-            else:
-                stress[step + 1, f, c, 2 + row] = value
 
         for row in rows:
             ap, lam, mu2 = coef[0, row], coef[3, row], coef[4, row]
@@ -379,11 +421,17 @@
                 dil = lam * d_p[1]
                 put(TT, row, part_s[f, TT, row] + dil)
                 put(TP, row, part_s[f, TP, row] + half * d_p[0])
-                if not last:
-                    put(TR, row, part_s[f, TR, row])
+                put(TR, row, part_s[f, TR, row])
             put(PP, row, part_s[f, PP, row] + (dil + mu2 * d_p[1]))
             put(RR, row, part_s[f, RR, row] + dil)
             put(PR, row, part_s[f, PR, row] + half * d_p[2])
+        if last:
+            finals = {(c, row): zone_or(STATE_OF[c], f, row, value) for (c, row), value in done.items()}
+            for (c, row), value in finals.items():
+                state_o[f, pl.ds(STATE_OF[c] * (LEV * ROWS) + row, LEV, stride=ROWS), :] = value
+        else:
+            for (c, row), value in done.items():
+                stress[step + 1, f, c, 2 + row] = value
         return done
 
     def edges_stress(step, f):
@@ -397,21 +445,22 @@
         return rims, copies
 
     def materials():
-        def body(row, carry):
-            ids = ids_in[pl.ds(row, LEV, stride=ROWS), :]
-            rho = jnp.zeros((LEV, LANES), F32)
+        def body(i, carry):
+            own = pl.ds(i * CHUNK, CHUNK)
+            ids = jnp.stack([ids_in[pl.ds(i * CHUNK + k, LEV, stride=ROWS), :] for k in range(CHUNK)])
+            rho = jnp.zeros((CHUNK, LEV, LANES), F32)
             lam, mu = rho, rho
             for layer in range(16):
                 hit = ids == layer
                 rho = jnp.where(hit, density_ref[layer], rho)
                 lam = jnp.where(hit, lame_ref[layer], lam)
                 mu = jnp.where(hit, shear_ref[layer], mu)
-            coef[2, row] = step_size * (1.0 / rho)
-            coef[3, row] = step_size * lam
-            coef[4, row] = (2.0 * step_size) * mu
+            coef[2, own] = step_size * (1.0 / rho)
+            coef[3, own] = step_size * lam
+            coef[4, own] = (2.0 * step_size) * mu
             return carry
 
-        lax.fori_loop(0, ROWS, body, 0)
+        lax.fori_loop(0, ROWS // CHUNK, body, 0)
         packed = (
             pack_rim(blank, INNER, lambda c, row: coef[2, row] * coef[0, row]),
             pack_rim(
@@ -464,11 +513,250 @@
                     total = piece if total is None else total + piece
                 inject[step, c] = total.reshape(ROWS, LEV, LANES)
 
+    ZROWS = 2 * ROWS
+    side = lax.rem(lane, 64)
+    own_at = 16 * is_e
+    strip_at = 8 + 8 * is_e
+    own_side = (side >= own_at) & (side < own_at + 16)
+    own_slot = lax.div(lax.rem(lane - own_at + 64, 64), 16)
+    strip_slot = lax.div(lax.rem(lane - strip_at + 64, 64), 8)
+
+    def pack_channel(ch, rows_of):
+        strips = [jnp.zeros((LEV, LANES), F32)] * 2
+        owns = [[jnp.zeros((LEV, LANES), F32)] * 2 for _ in range(2)]
+        window = []
+        for row in range(ROWS):
+            h, q = divmod(row, 8)
+            fwd, adj = rows_of(row)
+            both = jnp.where(lane < 64, lane_roll(fwd, 16), lane_roll(adj, 80))
+            window.append(both)
+            moved = lane_roll(both, 8 * q) if q else both
+            strips[h] = jnp.where(strip_slot == q, moved, strips[h])
+            moved = lane_roll(both, 16 * (q % 4)) if q % 4 else both
+            owns[h][q // 4] = jnp.where(own_slot == q % 4, moved, owns[h][q // 4])
+        for row in range(ROWS):
+            zone[ch, 2 + 8 + row] = window[row]
+        for h in range(2):
+            strip_pack[h, ch] = strips[h]
+            for g in range(2):
+                own_pack[h, ch, g] = owns[h][g]
+
+    def zone_pack_strips():
+        def body(ch, carry):
+            def rows_of(row):
+                rows = pl.ds(ch * (LEV * ROWS) + row, LEV, stride=ROWS)
+                return state_in[0, rows, :], state_in[1, rows, :]
+
+            pack_channel(ch, rows_of)
+            return carry
+
+        lax.fori_loop(0, 9, body, 0)
+        pack_channel(9, lambda row: (ids_in[pl.ds(row, LEV, stride=ROWS), :].astype(F32),) * 2)
+
+    def zone_copy(kind):
+        src, dst, slot, peer = (
+            (own_pack.at[0], own_recv.at[1 - is_top], 1 - is_top, up),
+            (own_pack.at[1], own_recv.at[is_bot], is_bot, down),
+            (strip_pack, strip_mid, 2, across),
+            (strip_pack.at[0], strip_recv.at[1 - is_top], 4 - is_top, across_up),
+            (strip_pack.at[1], strip_recv.at[is_bot], 3 + is_bot, across_down),
+        )[kind]
+        return pltpu.make_async_remote_copy(
+            src_ref=src,
+            dst_ref=dst,
+            send_sem=zone_ssem.at[kind],
+            recv_sem=zone_rsem.at[slot],
+            device_id=peer,
+            device_id_type=MESH,
+        )
+
+    def zone_wait(slot):
+        ref = (own_recv.at[0], own_recv.at[1], strip_mid, strip_recv.at[0], strip_recv.at[1])[slot]
+        pltpu.make_async_remote_copy(
+            src_ref=ref,
+            dst_ref=ref,
+            send_sem=zone_ssem.at[slot],
+            recv_sem=zone_rsem.at[slot],
+            device_id=up,
+            device_id_type=MESH,
+        ).wait_recv()
+
+    def zone_start():
+        zone_pack_strips()
+
+        @pl.when(is_w == 1)
+        def _():
+            for kind in (2, 3, 4):
+                zone_copy(kind).start()
+
+    def zone_start_own():
+        zone_copy(0).start()
+        zone_copy(1).start()
+
+    def zone_receive():
+        for slot in (2, 3, 4):
+            zone_wait(slot)
+
+        @pl.when(is_e == 1)
+        def _():
+            for kind in (2, 3, 4):
+                zone_copy(kind).start()
+
+        for slot in (0, 1):
+            zone_wait(slot)
+        flips = (1.0 - 2.0 * is_top.astype(F32), 1.0 - 2.0 * is_bot.astype(F32))
+
+        def body(ch, carry):
+            middle = []
+            for row in range(ROWS):
+                h, q = divmod(row, 8)
+                strip = lane_roll(strip_mid[h, ch], -8 * q) if q else strip_mid[h, ch]
+                middle.append(jnp.where(own_side, zone[ch, 2 + 8 + row], strip))
+            for row in range(ROWS):
+                zone[ch, 2 + 8 + row] = middle[row]
+            turns = (ch < 2) | (ch == 7) | (ch == 8)
+            for slot, pole, first in ((0, is_top, 0), (1, is_bot, 24)):
+                flip = jnp.where(turns, flips[slot], 1.0)
+                values = []
+                for q in range(8):
+                    own = own_recv[slot, ch, q // 4]
+                    own = lane_roll(own, -16 * (q % 4)) if q % 4 else own
+                    strip = strip_recv[slot, ch]
+                    strip = lane_roll(strip, -8 * q) if q else strip
+                    values.append(jnp.where(own_side, own, strip) * flip)
+                for q in range(8):
+                    zone[ch, 2 + first + q] = jnp.where(pole == 1, values[7 - q], values[q])
+            return carry
+
+        lax.fori_loop(0, 10, body, 0)
+
+    def zone_wait_sends():
+        for kind in range(5):
+            zone_copy(kind).wait_send()
+
+    def zone_cells():
+        row = lax.broadcasted_iota(jnp.int32, (ZROWS, LEV, LANES), 0) + (lat * ROWS - 8)
+        col = lax.broadcasted_iota(jnp.int32, (ZROWS, LEV, LANES), 2) + (lon * LANES + 112 - 128 * is_e + lon_cells)
+        turned = (row < 0) | (row >= lat_cells)
+        row = jnp.where(row < 0, -1 - row, jnp.where(row >= lat_cells, 2 * lat_cells - 1 - row, row))
+        col = lax.rem(col + jnp.where(turned, lon_cells // 2, 0), lon_cells)
+        return row, col
+
+    def zone_metrics():
+        row = lax.broadcasted_iota(jnp.int32, (ZROWS, LEV, LANES), 0) + (lat * ROWS - 8)
+        beyond = (row < 0) | (row >= lat_cells)
+        row = jnp.where(row < 0, -1 - row, jnp.where(row >= lat_cells, 2 * lat_cells - 1 - row, row))
+        theta = (row.astype(F32) + 0.5) * theta_step
+        sines = jnp.maximum(jnp.sin(theta), SIN_FLOOR) * jnp.where(beyond, -1.0, 1.0)
+        zcoef[0] = ir[None] / (sines * (12.0 * phi_step))
+        zcoef[1] = jnp.cos(theta) / sines * ir[None]
+
+    def zone_materials():
+        def body(i, carry):
+            row = pl.ds(2 + i * CHUNK, CHUNK)
+            ids = zone[9, pl.ds(4 + i * CHUNK, CHUNK)].astype(jnp.int32)
+            rho = jnp.ones((CHUNK, LEV, LANES), F32)
+            lam, mu = rho, rho
+            for layer in range(16):
+                hit = ids == layer
+                rho = jnp.where(hit, density_ref[layer], rho)
+                lam = jnp.where(hit, lame_ref[layer], lam)
+                mu = jnp.where(hit, shear_ref[layer], mu)
+            zcoef[2, row] = step_size * (1.0 / rho)
+            zcoef[3, row] = step_size * lam
+            zcoef[4, row] = (2.0 * step_size) * mu
+            return carry
+
+        lax.fori_loop(0, (ZROWS - 4) // CHUNK, body, 0)
+
+    def zone_injection():
+        plane = lat_cells * lon_cells
+        row, col = zone_cells()
+        level3 = lax.broadcasted_iota(jnp.int32, (ZROWS, LEV, LANES), 1)
+        lane3 = lax.broadcasted_iota(jnp.int32, (ZROWS, LEV, LANES), 2)
+        cell = jnp.where(lane3 < 32, level3 * plane + row * lon_cells + col, -1)
+        cells = cells_ref[...].reshape(1, -1)
+        count = cells.shape[1]
+        lev_n = lax.div(cells, plane)
+        in_plane = cells - lev_n * plane
+        row_n = lax.div(in_plane, lon_cells)
+        first = lon * LANES + 112 - 128 * is_e
+        col_n = lax.rem(in_plane - row_n * lon_cells - first + 2 * lon_cells, lon_cells)
+        over_n = lax.rem(col_n + lon_cells // 2, lon_cells)
+        straight = row_n - (lat * ROWS - 8)
+        turned = jnp.where(row_n < 8, 7 - row_n, lat_cells - 1 - row_n + 24)
+        can_turn = ((row_n < 8) & (is_top == 1)) | ((row_n >= lat_cells - 8) & (is_bot == 1))
+        is_turned = can_turn & (over_n < 32)
+        is_straight = (straight >= 0) & (straight < ZROWS) & (col_n < 32)
+        zrow_n = jnp.where(is_turned, turned, straight)
+        zcol_n = jnp.where(is_turned, over_n, col_n) + 64
+        place_n = jnp.where(is_turned | is_straight, zrow_n * LEV + lev_n, -1)
+        sign_n = jnp.where(is_turned, -1.0, 1.0)
+        index = lax.broadcasted_iota(jnp.int32, (LANES, count), 0)
+        lane_hot = jnp.where(index == zcol_n, 1.0, 0.0).astype(jnp.bfloat16)
+        for part in range(2):
+            place_hit = index + part * LANES == place_n
+            for step in range(STEPS):
+                for c in range(3):
+                    values = resid_ref[c, pl.ds(step, 1)]
+                    if c < 2:
+                        values = values * sign_n
+                    high = values.astype(jnp.bfloat16).astype(F32)
+                    rest = values - high
+                    middle = rest.astype(jnp.bfloat16).astype(F32)
+                    total = None
+                    for term in (high, middle, rest - middle):
+                        left_hot = jnp.where(place_hit, term, 0.0).astype(jnp.bfloat16)
+                        piece = lax.dot_general(
+                            left_hot, lane_hot, (((1,), (1,)), ((), ())), preferred_element_type=F32
+                        )
+                        total = piece if total is None else total + piece
+                    zinject[step, c, part * ROWS : (part + 1) * ROWS] = total.reshape(ROWS, LEV, LANES)
+        adds = [jnp.zeros((ZROWS, LEV, LANES), F32) for _ in range(STEPS)]
+        for s in range(src_ref.shape[0]):
+            hit = cell == src_ref[s]
+            for step in range(STEPS):
+                adds[step] = adds[step] + jnp.where(hit, wave_ref[step, s], 0.0)
+        for step in range(STEPS):
+            zinject[step, 2] += adds[step]
+
+    def zone_steps():
+        for step in range(STEPS):
+
+            def velocity_body(i, carry):
+                r0 = 2 + 4 * step + i * CHUNK
+                own = pl.ds(r0, CHUNK)
+                scale = zcoef[2, own]
+                for c, force in enumerate(force_terms(zone, STATE_OF, zcoef, r0)):
+                    zone[c, pl.ds(r0 + 2, CHUNK)] += scale * force + zinject[step, c, own]
+                return carry
+
+            lax.fori_loop(0, 7 - 2 * step, velocity_body, 0)
+            density = None
+            for c in range(3):
+                new = zone[c, 2 + 8 : 2 + 8 + ROWS]
+                term = new * lane_roll(new, 64)
+                density = term if density is None else density + term
+            zdensity[...] = density if step == 0 else zdensity[...] + density
+
+            def stress_body(i, carry):
+                r0 = 4 + 4 * step + i * CHUNK
+                for c, rate in enumerate(stress_terms(zone, zcoef, r0)):
+                    zone[STATE_OF[c], pl.ds(r0 + 2, CHUNK)] += rate
+                return carry
+
+            lax.fori_loop(0, 6 - 2 * step, stress_body, 0)
+
+    seam_side = (lane >= LANES * (1 - is_e) - 8 * is_w) & (lane < LANES - (LANES - 8) * is_e)
+
+    def zone_or(ch, f, row, value):
+        return jnp.where(seam_side, lane_roll(zone[ch, 2 + 8 + row], -16 - 64 * f), value)
+
     started = []
     for f in range(2):
         loads[f].wait()
         unpack_stress(f, range(3), BOUNDARY)
-    pl.semaphore_wait(barrier, 4)
+    pl.semaphore_wait(barrier, 4 - is_e + 2 * is_w)
     for f in range(2):
         started += send_cols(0, f, stress.at[0, f])
     for f in range(2):
@@ -477,42 +765,90 @@
         packed = pack_rim(blank, range(ROWS), lambda c, row: stress[0, f, TP + c, 2 + row])
         for group in range(2):
             lon_send[0, f, group] = packed[group]
-        started += send_lons(0, f)
+        send_lons(0, f)
     for load in loads[2:]:
         load.wait()
+
+    @pl.when(is_w == 1)
+    def _():
+        zone_start()
+
     materials()
     injection()
     for step in range(STEPS):
         for f in range(2):
             local_velocity(step, f)
+        if step == 1:
+
+            @pl.when(at_seam == 1)
+            def _():
+                zone_injection()
+
         rims = []
         for f in range(2):
             rim, copies = edges_velocity(step, f)
             rims.append(rim)
             started += copies
         for f in range(2):
-            finish_velocity(step, f, INNER, rims[f])
+            for rows in INNER_GROUPS:
+                finish_velocity(step, f, rows, rims[f])
             local_stress(step, f)
+        if step == 0:
+
+            @pl.when(is_e == 1)
+            def _():
+                zone_start()
+
+            @pl.when(at_seam == 1)
+            def _():
+                zone_start_own()
+                zone_metrics()
+
         if step == STEPS - 1:
+
+            @pl.when(at_seam == 1)
+            def _():
+                zone_receive()
+                zone_materials()
+                zone_steps()
+
+            densities = []
             for row in range(ROWS):
                 density = None
                 for s in range(STEPS):
                     for c in range(3):
                         term = vel[s, 0, c, 2 + row] * vel[s, 1, c, 2 + row]
                         density = term if density is None else density + term
-                kern_o[pl.ds(row, LEV, stride=ROWS), :] = density
-                for f in range(2):
-                    for c in range(3):
-                        state_o[f, pl.ds(c * (LEV * ROWS) + row, LEV, stride=ROWS), :] = vel[step, f, c, 2 + row]
+                densities.append(jnp.where(seam_side, lane_roll(zdensity[row], -16), density))
+            for row in range(ROWS):
+                kern_o[pl.ds(row, LEV, stride=ROWS), :] = densities[row]
+            for f in range(2):
+                for c in range(3):
+                    values = [zone_or(c, f, row, vel[step, f, c, 2 + row]) for row in range(ROWS)]
+                    for row in range(ROWS):
+                        state_o[f, pl.ds(c * (LEV * ROWS) + row, LEV, stride=ROWS), :] = values[row]
         rims = []
         for f in range(2):
             rim, copies = edges_stress(step, f)
             rims.append(rim)
             started += copies
         for f in range(2):
-            finish_stress(step, f, INNER, rims[f])
+            for rows in INNER_GROUPS:
+                finish_stress(step, f, rows, rims[f])
+
     for copy in started:
         copy.wait_send()
+    for phase in range(2 * STEPS):
+        for f in range(2):
+            for slot, seam in ((0, is_w), (1, is_e)):
+
+                @pl.when(seam == 0)
+                def _():
+                    lon_copy(phase, f, slot).wait_send()
+
+    @pl.when(at_seam == 1)
+    def _():
+        zone_wait_sends()
 
 
 def store(state_ref, kern_ref, fwd_out, adj_out, kern_out, sem):
@@ -553,11 +889,22 @@
             pltpu.VMEM((phases, 2, 2, 3, 2, LEV, LANES), F32),
             pltpu.VMEM((phases, 2, 2, LEV, LANES), F32),
             pltpu.VMEM((phases, 2, 2, 2, LEV, LANES), F32),
+            pltpu.VMEM((10, 2 * ROWS + 4, LEV, LANES), F32),
+            pltpu.VMEM((5, 2 * ROWS, LEV, LANES), F32),
+            pltpu.VMEM((STEPS, 3, 2 * ROWS, LEV, LANES), F32),
+            pltpu.VMEM((ROWS, LEV, LANES), F32),
+            pltpu.VMEM((2, 10, 2, LEV, LANES), F32),
+            pltpu.VMEM((2, 10, 2, LEV, LANES), F32),
+            pltpu.VMEM((2, 10, LEV, LANES), F32),
+            pltpu.VMEM((2, 10, LEV, LANES), F32),
+            pltpu.VMEM((2, 10, LEV, LANES), F32),
             pltpu.SemaphoreType.DMA((5,)),
             pltpu.SemaphoreType.DMA((phases, 2, 2)),
             pltpu.SemaphoreType.DMA((phases, 2, 2)),
             pltpu.SemaphoreType.DMA((phases, 2, 2)),
             pltpu.SemaphoreType.DMA((phases, 2, 2)),
+            pltpu.SemaphoreType.DMA((5,)),
+            pltpu.SemaphoreType.DMA((5,)),
         ],
         compiler_params=pltpu.CompilerParams(collective_id=0, has_side_effects=True),
         name="elastic_steps",

time: 42.4 us -> 39.6 us (0.934)
  the two profiles are of different devices: /device:TPU:8 before, /device:TPU:32 now
where the time goes in v3:
time: 39.6 us; the launch traced here: 39.4 us
  Pallas kernels  38.7 us (98%)
  between operations  0.64 us (2%)
    pallas_call x1, Pallas kernels, on_device(): pl.pallas_call(functools.partial(kernel, n_lon, n_lat), out_shape=(pltpu....  37.7 us
    pallas_call x1, Pallas kernels, on_device(): pl.pallas_call(store, out_shape=(jax.ShapeDtypeStruct((flat, LANES), F32)...  1.05 us

profile of v3, /device:TPU:32, one launch (start us, length us, event | category | flops | bytes accessed | tf_op | source)
XLA Modules:
  0.0 39.4 jit_solution(8179803062388197275)
XLA Ops:
  0.6 37.7 %elastic_steps.1 = (f32[2,1152,128]{2,1,0:T(8,128)S(1)}, f32[128,128]{1,0:T(8,128)S(1)}) custom-call(f32[1152,128]{1,0:T(8,128)} %bitcast.7, f32[1152,128]{1,0:T(8,128)} %bitcast.8, s32[128,128]{1,0:T(8,128)} %bitcast.9, f32[16]{0:T(128)} %density_ref.1, f32[16]{0:T(128)} %lame_ref.1, f32[16]{0:T(128)} %shear_ref.1, s32[8]{0:T(128)} %src_ref.1, ...), custom_call_target="tpu_custom_call" | custom-call | tf_op jit(solution)/shard_map/elastic_steps/pallas_call | solution.py:872
  38.3 1.0 %store.1 = (f32[1152,128]{1,0:T(8,128)}, f32[1152,128]{1,0:T(8,128)}, f32[128,128]{1,0:T(8,128)}) custom-call(f32[2,1152,128]{2,1,0:T(8,128)S(1)} %get-tuple-element.8.state_ref, f32[128,128]{1,0:T(8,128)S(1)} %get-tuple-element.9.kern_ref), custom_call_target="tpu_custom_call" | custom-call | tf_op jit(solution)/shard_map/store/pallas_call | solution.py:923

commit v4 on v3

--- a/solution.py
+++ b/solution.py
@@ -473,6 +473,17 @@
             for group in range(2):
                 coef_rim[kind, group] = packed[kind][group]
 
+    def spread(values, place_hit, lane_hot):
+        high = values.astype(jnp.bfloat16).astype(F32)
+        rest = values - high
+        middle = rest.astype(jnp.bfloat16).astype(F32)
+        total = None
+        for term in (high, middle, rest - middle):
+            left_hot = jnp.where(place_hit, term, 0.0).astype(jnp.bfloat16)
+            piece = lax.dot_general(left_hot, lane_hot, (((1,), (1,)), ((), ())), preferred_element_type=F32)
+            total = piece if total is None else total + piece
+        return total.reshape(ROWS, LEV, LANES)
+
     def injection():
         plane = lat_cells * lon_cells
         rows = lax.broadcasted_iota(jnp.int32, (ROWS, LEV, LANES), 0) + lat * ROWS
@@ -498,20 +509,13 @@
         index = lax.broadcasted_iota(jnp.int32, (LANES, count), 0)
         lane_hot = jnp.where(index == col_n, 1.0, 0.0).astype(jnp.bfloat16)
         place_hit = index == place_n
-        for step in range(STEPS):
-            for c in range(3):
-                values = resid_ref[c, pl.ds(step, 1)]
-                high = values.astype(jnp.bfloat16).astype(F32)
-                rest = values - high
-                middle = rest.astype(jnp.bfloat16).astype(F32)
-                total = None
-                for term in (high, middle, rest - middle):
-                    left_hot = jnp.where(place_hit, term, 0.0).astype(jnp.bfloat16)
-                    piece = lax.dot_general(
-                        left_hot, lane_hot, (((1,), (1,)), ((), ())), preferred_element_type=F32
-                    )
-                    total = piece if total is None else total + piece
-                inject[step, c] = total.reshape(ROWS, LEV, LANES)
+
+        def body(c, carry):
+            for step in range(STEPS):
+                inject[step, c] = spread(resid_ref[c, pl.ds(step, 1)], place_hit, lane_hot)
+            return carry
+
+        lax.fori_loop(0, 3, body, 0)
 
     ZROWS = 2 * ROWS
     side = lax.rem(lane, 64)
@@ -696,22 +700,15 @@
         lane_hot = jnp.where(index == zcol_n, 1.0, 0.0).astype(jnp.bfloat16)
         for part in range(2):
             place_hit = index + part * LANES == place_n
-            for step in range(STEPS):
-                for c in range(3):
-                    values = resid_ref[c, pl.ds(step, 1)]
-                    if c < 2:
-                        values = values * sign_n
-                    high = values.astype(jnp.bfloat16).astype(F32)
-                    rest = values - high
-                    middle = rest.astype(jnp.bfloat16).astype(F32)
-                    total = None
-                    for term in (high, middle, rest - middle):
-                        left_hot = jnp.where(place_hit, term, 0.0).astype(jnp.bfloat16)
-                        piece = lax.dot_general(
-                            left_hot, lane_hot, (((1,), (1,)), ((), ())), preferred_element_type=F32
-                        )
-                        total = piece if total is None else total + piece
-                    zinject[step, c, part * ROWS : (part + 1) * ROWS] = total.reshape(ROWS, LEV, LANES)
+            signs = sign_n
+
+            def body(c, carry):
+                for step in range(STEPS):
+                    values = resid_ref[c, pl.ds(step, 1)] * jnp.where(c < 2, signs, 1.0)
+                    zinject[step, c, part * ROWS : (part + 1) * ROWS] = spread(values, place_hit, lane_hot)
+                return carry
+
+            lax.fori_loop(0, 3, body, 0)
         adds = [jnp.zeros((ZROWS, LEV, LANES), F32) for _ in range(STEPS)]
         for s in range(src_ref.shape[0]):
             hit = cell == src_ref[s]

time: 39.6 us -> 39.6 us (level)
  no operation moved by 1% of the time
where the time goes in v4:
time: 39.6 us; the launch traced here: 39.4 us
  Pallas kernels  38.7 us (98%)
  between operations  0.64 us (2%)
    pallas_call x1, Pallas kernels, on_device(): pl.pallas_call(functools.partial(kernel, n_lon, n_lat), out_shape=(pltpu....  37.7 us
    pallas_call x1, Pallas kernels, on_device(): pl.pallas_call(store, out_shape=(jax.ShapeDtypeStruct((flat, LANES), F32)...  1.05 us

profile of v4, /device:TPU:32, one launch (start us, length us, event | category | flops | bytes accessed | tf_op | source)
XLA Modules:
  0.0 39.4 jit_solution(10838776170405054843)
XLA Ops:
  0.6 37.7 %elastic_steps.1 = (f32[2,1152,128]{2,1,0:T(8,128)S(1)}, f32[128,128]{1,0:T(8,128)S(1)}) custom-call(f32[1152,128]{1,0:T(8,128)} %bitcast.7, f32[1152,128]{1,0:T(8,128)} %bitcast.8, s32[128,128]{1,0:T(8,128)} %bitcast.9, f32[16]{0:T(128)} %density_ref.1, f32[16]{0:T(128)} %lame_ref.1, f32[16]{0:T(128)} %shear_ref.1, s32[8]{0:T(128)} %src_ref.1, ...), custom_call_target="tpu_custom_call" | custom-call | tf_op jit(solution)/shard_map/elastic_steps/pallas_call | solution.py:869
  38.3 1.0 %store.1 = (f32[1152,128]{1,0:T(8,128)}, f32[1152,128]{1,0:T(8,128)}, f32[128,128]{1,0:T(8,128)}) custom-call(f32[2,1152,128]{2,1,0:T(8,128)S(1)} %get-tuple-element.8.state_ref, f32[128,128]{1,0:T(8,128)S(1)} %get-tuple-element.9.kern_ref), custom_call_target="tpu_custom_call" | custom-call | tf_op jit(solution)/shard_map/store/pallas_call | solution.py:920
